TPU v7x, 256 devices: a whole 4x4x8 slice. The times are simulated.
256 devices in a mesh: dp: 8 (over y, core), expert: 32 (over x, z).
Axes of the slice: x: 4, y: 4, z: 8, core: 2. Of those that a mesh axis runs over, the one named last changes fastest.
Arguments:
- tokens: bfloat16 [2048, 4096], P(('dp', 'expert')), may hold values from -6 to 6
- expert_ids: int32 [2048, 8], P(('dp', 'expert')), may hold values from 0 to 31, all different within a row; in each aligned block of 8 rows (0 to 7, 8 to 15, ...) at most 3 rows name the same one
- gate_values: float32 [2048, 8], P(('dp', 'expert')), may hold values from 0.05 to 1
- w_gate: bfloat16 [32, 4096, 2048], P('expert', None, 'dp'), may hold values from -0.09375 to 0.09375
- w_up: bfloat16 [32, 4096, 2048], P('expert', None, 'dp'), may hold values from -0.09375 to 0.09375
- w_down: bfloat16 [32, 2048, 4096], P('expert', 'dp'), may hold values from -0.125 to 0.125
- s_gate: bfloat16 [4096, 2048], P(None, 'dp'), may hold values from -0.09375 to 0.09375
- s_up: bfloat16 [4096, 2048], P(None, 'dp'), may hold values from -0.09375 to 0.09375
- s_down: bfloat16 [2048, 4096], P('dp'), may hold values from -0.125 to 0.125
Outputs:
- mixed: bfloat16 [2048, 4096], P(('dp', 'expert'))
Inputs may be any that keep to these rules, and one draw needn't show every extreme that they name: `expert_ids`: each row names 8 different experts; the 8 rows of one device name one expert at most 3 times.
All inputs are finite; a program needn't handle non-finite values.
Results may differ from a plain program's by a relative error of at most 0.0054.
Values may be sent and summed in bfloat16 or wider, within the bound.
No kernel may reach another device: no remote copies, remote signals or barrier semaphores. Data moves between devices by JAX's collectives and lax.ppermute only.
A program may use at most 128 MiB of HBM per device.

v0:
```python
import jax
import jax.numpy as jnp
from jax import lax
from jax.experimental import pallas as pl
from jax.experimental.pallas import tpu as pltpu
from jax.sharding import Mesh, PartitionSpec as P

CAP = 3
PARTS = 1
LANES = 128
SMALL = pltpu.CompilerParams(vmem_limit_bytes=6 * 2**20)


def in_smem():
    return pl.BlockSpec(memory_space=pltpu.SMEM)


def in_vmem():
    return pl.BlockSpec(memory_space=pltpu.VMEM)


def pack_rows(ids, rows3, experts):
    count, picks = ids.shape

    def kernel(ids_ref, rows_ref, out_ref, slot_ref, used_ref):
        out_ref[...] = jnp.zeros_like(out_ref)
        for e in range(experts):
            used_ref[e] = 0
        for r in range(count):
            row = rows_ref[r]
            for k in range(picks):
                e = ids_ref[r, k]
                n = used_ref[e]
                used_ref[e] = n + 1
                slot = e * CAP + n
                slot_ref[r, k] = slot
                out_ref[slot] = row

    return pl.pallas_call(
        kernel,
        out_shape=(
            jax.ShapeDtypeStruct((experts * CAP,) + rows3.shape[1:], rows3.dtype),
            jax.ShapeDtypeStruct(ids.shape, jnp.int32),
        ),
        in_specs=[in_smem(), in_vmem()],
        out_specs=(in_vmem(), in_smem()),
        scratch_shapes=[pltpu.SMEM((experts,), jnp.int32)],
        compiler_params=SMALL,
        name="pack_rows",
    )(ids, rows3)


def combine_rows(slots, gates, shared3, *returned):
    count, picks = slots.shape
    folds = shared3.shape[1] // len(returned)

    def kernel(slot_ref, gates_ref, shared_ref, *refs):
        out_ref = refs[-1]
        for index, ret_ref in enumerate(refs[:-1]):
            part = slice(index * folds, (index + 1) * folds)
            for r in range(count):
                total = shared_ref[r, part]
                for k in range(picks):
                    total = total + gates_ref[r, k] * ret_ref[slot_ref[r, k]].astype(jnp.float32)
                out_ref[r, part] = total.astype(out_ref.dtype)

    return pl.pallas_call(
        kernel,
        out_shape=jax.ShapeDtypeStruct(shared3.shape, jnp.bfloat16),
        in_specs=[in_smem(), in_smem(), in_vmem()] + [in_vmem() for _ in returned],
        out_specs=in_vmem(),
        compiler_params=SMALL,
        name="combine_rows",
    )(slots, gates, shared3, *returned)


def hidden_of(rows, gate_w, up_w):
    gate = jnp.dot(rows, gate_w, preferred_element_type=jnp.float32)
    up = jnp.dot(rows, up_w, preferred_element_type=jnp.float32)
    return lax.optimization_barrier((jax.nn.silu(gate) * up).astype(jnp.bfloat16))


def down(hidden, down_w):
    return jnp.dot(hidden, down_w, preferred_element_type=jnp.float32)


def shift(value, axis, by):
    n = lax.axis_size(axis)
    return lax.ppermute(value, axis, [(i, (i + by) % n) for i in range(n)])


def layer(tokens, ids, gates, w_gate, w_up, w_down, s_gate, s_up, s_down):
    experts = lax.axis_size(("x", "z"))
    planes = lax.axis_size("y")
    own, width = tokens.shape
    folds = width // LANES
    slots = experts * CAP
    half = slots // 2

    def exchange(rows, part):
        split = (experts, CAP, part, LANES)
        arrived = lax.all_to_all(rows.reshape(split), ("x", "z"), split_axis=0, concat_axis=0, tiled=True)
        return arrived.reshape(slots, part, LANES)

    packed, places = pack_rows(ids, tokens.reshape(own, folds, LANES), experts)
    early, packed = lax.optimization_barrier((tokens, packed))

    own_w = (w_gate[0], w_up[0], w_down[0])
    other_w = [shift(w, "core", 1) for w in own_w]
    gate_w, up_w = (jnp.concatenate(pair, axis=1) for pair in zip(own_w[:2], other_w[:2]))
    step = width // PARTS
    down_w = [
        jnp.concatenate([w[:, part * step : (part + 1) * step] for w in (own_w[2], other_w[2])], axis=0)
        for part in range(PARTS)
    ]

    arrived = exchange(packed, folds)

    column = jnp.concatenate([early] + [shift(early, "y", by) for by in range(1, planes)], axis=0)
    column = jnp.concatenate([column, shift(column, "core", 1)], axis=0)
    shared_part = down(hidden_of(column, s_gate, s_up), s_down)
    rows = planes * own
    back = shift(shared_part[rows:].astype(jnp.bfloat16), "core", 1)
    shared_part = (shared_part[:rows] + back.astype(jnp.float32)).reshape(planes, own, width)
    shared = shared_part[0]
    for by in range(1, planes):
        back = shift(shared_part[by].astype(jnp.bfloat16), "y", planes - by)
        shared = shared + back.astype(jnp.float32)

    gate_w, up_w, *down_w = lax.optimization_barrier((gate_w, up_w, *down_w))

    mine = arrived.reshape(slots, width)
    left, right = shift(mine, "y", 1), shift(mine, "y", planes - 1)
    far = [shift(left[:half], "y", 1), shift(right[half:], "y", planes - 1)]
    far = jnp.concatenate(far, axis=0)

    own_hidden = hidden_of(mine, gate_w, up_w)
    total = [down(own_hidden, w) for w in down_w]
    near_hidden = hidden_of(jnp.concatenate([left, right], axis=0), gate_w, up_w)
    near = [down(near_hidden, w).astype(jnp.bfloat16) for w in down_w]
    far_hidden = hidden_of(far, gate_w, up_w)
    far = [down(far_hidden, w).astype(jnp.bfloat16) for w in down_w]

    returned = []
    for part in range(PARTS):
        back = [shift(near[part][:slots], "y", planes - 1), shift(near[part][slots:], "y", 1)]
        back.append(shift(far[part], "y", 2))
        for value in back:
            total[part] = total[part] + value.astype(jnp.float32)
        returned.append(exchange(total[part].astype(jnp.bfloat16), folds // PARTS))

    mixed = combine_rows(places, gates, shared.reshape(own, folds, LANES), *returned)
    return mixed.reshape(own, width)


def solution(mesh):
    fine = Mesh(mesh.devices.reshape(4, 2, 4, 8), ("y", "core", "x", "z"))
    dp, expert = ("y", "core"), ("x", "z")
    placed = (
        P(dp + expert, None),
        P(dp + expert, None),
        P(dp + expert, None),
        P(expert, None, dp),
        P(expert, None, dp),
        P(expert, dp, None),
        P(None, dp),
        P(None, dp),
        P(dp, None),
    )
    return jax.shard_map(layer, mesh=fine, in_specs=placed, out_specs=P(dp + expert, None), check_vma=False)
```

profile of v0, /device:TPU:2, one launch (start us, length us, event | category | flops | bytes accessed | tf_op | source)
XLA Modules:
  0.0 135.1 jit_solution(15670296331814870895)
XLA Ops:
  1.7 1.8 %pack_rows.1 = (bf16[96,32,128]{2,1,0:T(8,128)(2,1)}, s32[8,8]{1,0:T(8,128)S(1)}) custom-call(s32[8,8]{1,0:T(8,128)S(1)} %copy-done.2, bf16[8,32,128]{2,1,0:T(8,128)(2,1)S(1)} %bitcast.53), custom_call_target="tpu_custom_call" | custom-call | tf_op jit(solution)/shard_map/pack_rows/pallas_call | solution.py:39
  3.5 3.1 %collective-permute-start.2 = (bf16[8,4096]{1,0:T(8,128)(2,1)}, bf16[8,4096]{1,0:T(8,128)(2,1)S(1)}, u32[]{:S(2)}, u32[]{:S(2)}) collective-permute-start(bf16[8,4096]{1,0:T(8,128)(2,1)} %param.9), channel_id=1, source_target_pairs={{0,192},{64,0},{128,64},{192,128},{1,193},{65,1},{129,65},{193,129... | collective-permute-start | bytes 196616 | tf_op jit(solution)/shard_map/ppermute | solution.py:89
  8.2 11.6 %all-to-all-start = ((bf16[32,3,32,128]{3,2,1,0:T(8,128)(2,1)}), bf16[32,3,32,128]{3,2,1,0:T(8,128)(2,1)S(1)}, u32[]{:S(2)}, u32[]{:S(2)}) async-start(bf16[32,3,32,128]{3,2,1,0:T(8,128)(2,1)} %bitcast), calls=%async_computation | async-start | bytes 1572864 | tf_op jit(solution)/shard_map/all_to_all | solution.py:102
  22.9 7.9 %collective-permute-done.3 = bf16[32,4096]{1,0:T(8,128)(2,1)S(1)} collective-permute-done((bf16[32,4096]{1,0:T(8,128)(2,1)S(1)}, bf16[32,4096]{1,0:T(8,128)(2,1)S(1)}, u32[]{:S(2)}, u32[]{:S(2)}) %collective-permute-start.3) | collective-permute-done | bytes 262176 | tf_op jit(solution)/shard_map/ppermute | solution.py:89
  30.7 2.1 %fusion.9 = f32[64,256]{1,0:T(8,128)S(1)} fusion(bf16[64,4096]{1,0:T(8,128)(2,1)S(1)} %constant_dynamic-update-slice_fusion, bf16[4096,256]{1,0:T(8,128)(2,1)} %param.15), kind=kOutput, calls=%fused_computation.36 | convolution fusion | flops 134217728 | bytes 2686976 | tf_op jit(solution)/shard_map/dot_general | solution.py:78
  33.3 6.5 %all-to-all-done = bf16[32,3,32,128]{3,2,1,0:T(8,128)(2,1)S(1)} async-done(((bf16[32,3,32,128]{3,2,1,0:T(8,128)(2,1)}), bf16[32,3,32,128]{3,2,1,0:T(8,128)(2,1)S(1)}, u32[]{:S(2)}, u32[]{:S(2)}) %all-to-all-start) | async-done | bytes 786464 | tf_op jit(solution)/shard_map/all_to_all | solution.py:102
  40.1 2.3 %collective-permute-start.12 = (bf16[96,4096]{1,0:T(8,128)(2,1)S(1)}, bf16[96,4096]{1,0:T(8,128)(2,1)S(1)}, u32[]{:S(2)}, u32[]{:S(2)}) collective-permute-start(bf16[96,4096]{1,0:T(8,128)(2,1)S(1)} %bitcast.65), channel_id=1, source_target_pairs={{0,192},{64,0},{128,64},{192,128},{1,193},{65,1},{129,65},{193,129... | collective-permute-start | bytes 2359304 | tf_op jit(solution)/shard_map/ppermute | solution.py:89
  42.5 2.5 %pad_maximum_fusion = bf16[4096,512]{1,0:T(8,128)(2,1)S(1)} fusion(bf16[4096,256]{1,0:T(8,128)(2,1)} %collective-permute-done.8, bf16[4096,256]{1,0:T(8,128)(2,1)} %bitcast.60), kind=kLoop, calls=%fused_computation.2 | loop fusion | flops 8388608 | bytes 8388608 | tf_op jit(solution)/shard_map/concatenate | solution.py:110
  45.0 2.0 %pad_maximum_fusion.1 = bf16[4096,512]{1,0:T(8,128)(2,1)S(1)} fusion(bf16[4096,256]{1,0:T(8,128)(2,1)} %collective-permute-done.9, bf16[4096,256]{1,0:T(8,128)(2,1)S(1)} %bitcast.62), kind=kLoop, calls=%fused_computation.3 | loop fusion | flops 8388608 | bytes 8388608 | tf_op jit(solution)/shard_map/concatenate | solution.py:110
  47.2 2.1 %pad_maximum_fusion.2 = bf16[512,4096]{1,0:T(8,128)(2,1)S(1)} fusion(bf16[256,4096]{1,0:T(8,128)(2,1)} %collective-permute-done.10, bf16[256,4096]{1,0:T(8,128)(2,1)S(1)} %bitcast.64), kind=kLoop, calls=%fused_computation.4 | loop fusion | flops 8388608 | bytes 8388608 | tf_op jit(solution)/shard_map/concatenate | solution.py:113
  49.3 8.5 %collective-permute-done.12 = bf16[96,4096]{1,0:T(8,128)(2,1)S(1)} collective-permute-done((bf16[96,4096]{1,0:T(8,128)(2,1)S(1)}, bf16[96,4096]{1,0:T(8,128)(2,1)S(1)}, u32[]{:S(2)}, u32[]{:S(2)}) %collective-permute-start.12) | collective-permute-done | bytes 786464 | tf_op jit(solution)/shard_map/ppermute | solution.py:89
  57.8 2.3 %collective-permute-start.16 = (bf16[48,4096]{1,0:T(8,128)(2,1)S(1)}, bf16[48,4096]{1,0:T(8,128)(2,1)S(1)}, u32[]{:S(2)}, u32[]{:S(2)}) collective-permute-start(bf16[48,4096]{1,0:T(8,128)(2,1)S(1)} %slice.57), channel_id=1, source_target_pairs={{0,192},{64,0},{128,64},{192,128},{1,193},{65,1},{129,65},{193,129... | collective-permute-start | bytes 1179656 | tf_op jit(solution)/shard_map/ppermute | solution.py:89
  63.7 3.3 %collective-permute-start.13 = (bf16[96,4096]{1,0:T(8,128)(2,1)S(1)}, bf16[96,4096]{1,0:T(8,128)(2,1)S(1)}, u32[]{:S(2)}, u32[]{:S(2)}) collective-permute-start(bf16[96,4096]{1,0:T(8,128)(2,1)S(1)} %get-tuple-element.21), channel_id=1, source_target_pairs={{0,192},{64,0},{128,64},{192,128},{1,193},{65,1},{129,65},{193,129... | collective-permute-start | bytes 2359304 | tf_op jit(solution)/shard_map/ppermute | solution.py:89
  67.0 6.6 %collective-permute-done.15 = bf16[48,4096]{1,0:T(8,128)(2,1)S(1)} collective-permute-done((bf16[48,4096]{1,0:T(8,128)(2,1)S(1)}, bf16[48,4096]{1,0:T(8,128)(2,1)S(1)}, u32[]{:S(2)}, u32[]{:S(2)}) %collective-permute-start.15) | collective-permute-done | bytes 393248 | tf_op jit(solution)/shard_map/ppermute | solution.py:89
  78.7 19.1 %collective-permute-done.13 = bf16[96,4096]{1,0:T(8,128)(2,1)S(1)} collective-permute-done((bf16[96,4096]{1,0:T(8,128)(2,1)S(1)}, bf16[96,4096]{1,0:T(8,128)(2,1)S(1)}, u32[]{:S(2)}, u32[]{:S(2)}) %collective-permute-start.13) | collective-permute-done | bytes 786464 | tf_op jit(solution)/shard_map/ppermute | solution.py:89
  97.8 3.4 %collective-permute-done.14 = bf16[96,4096]{1,0:T(8,128)(2,1)S(1)} collective-permute-done((bf16[96,4096]{1,0:T(8,128)(2,1)S(1)}, bf16[96,4096]{1,0:T(8,128)(2,1)S(1)}, u32[]{:S(2)}, u32[]{:S(2)}) %collective-permute-start.14) | collective-permute-done | bytes 786464 | tf_op jit(solution)/shard_map/ppermute | solution.py:89
  101.3 1.2 fusion.1
  103.6 12.9 %all-to-all-start.1 = ((bf16[32,3,32,128]{3,2,1,0:T(8,128)(2,1)}), bf16[32,3,32,128]{3,2,1,0:T(8,128)(2,1)S(1)}, u32[]{:S(2)}, u32[]{:S(2)}) async-start(bf16[32,3,32,128]{3,2,1,0:T(8,128)(2,1)} %bitcast.58), calls=%async_computation.1 | async-start | bytes 1572864 | tf_op jit(solution)/shard_map/all_to_all | solution.py:102
  116.5 1.1 fusion.6
  117.7 2.0 %collective-permute-start.7 = (bf16[8,4096]{1,0:T(8,128)(2,1)S(1)}, bf16[8,4096]{1,0:T(8,128)(2,1)S(1)}, u32[]{:S(2)}, u32[]{:S(2)}) collective-permute-start(bf16[8,4096]{1,0:T(8,128)(2,1)S(1)} %get-tuple-element.24), channel_id=1, source_target_pairs={{0,64},{64,128},{128,192},{192,0},{1,65},{65,129},{129,193},{193,1... | collective-permute-start | bytes 196616 | tf_op jit(solution)/shard_map/ppermute | solution.py:89
  120.3 1.7 %collective-permute-done.5 = bf16[8,4096]{1,0:T(8,128)(2,1)S(1)} collective-permute-done((bf16[8,4096]{1,0:T(8,128)(2,1)S(1)}, bf16[8,4096]{1,0:T(8,128)(2,1)S(1)}, u32[]{:S(2)}, u32[]{:S(2)}) %collective-permute-start.5) | collective-permute-done | bytes 65568 | tf_op jit(solution)/shard_map/ppermute | solution.py:89
  122.0 1.3 collective-permute-done.7
  123.3 2.2 %collective-permute-done.6 = bf16[8,4096]{1,0:T(8,128)(2,1)S(1)} collective-permute-done((bf16[8,4096]{1,0:T(8,128)(2,1)S(1)}, bf16[8,4096]{1,0:T(8,128)(2,1)S(1)}, u32[]{:S(2)}, u32[]{:S(2)}) %collective-permute-start.6) | collective-permute-done | bytes 65568 | tf_op jit(solution)/shard_map/ppermute | solution.py:89
  125.6 8.0 %all-to-all-done.1 = bf16[32,3,32,128]{3,2,1,0:T(8,128)(2,1)S(1)} async-done(((bf16[32,3,32,128]{3,2,1,0:T(8,128)(2,1)}), bf16[32,3,32,128]{3,2,1,0:T(8,128)(2,1)S(1)}, u32[]{:S(2)}, u32[]{:S(2)}) %all-to-all-start.1) | async-done | bytes 786464 | tf_op jit(solution)/shard_map/all_to_all | solution.py:102
  (69 shorter events, 19.0 us)
Async XLA Ops:
  0.0 76.7 %copy-start = (bf16[256,4096]{1,0:T(8,128)(2,1)S(1)}, bf16[256,4096]{1,0:T(8,128)(2,1)}, u32[]{:S(2)}) copy-start(bf16[256,4096]{1,0:T(8,128)(2,1)} %param.17) | copy-start | bytes 6291460
  3.5 17.8 %collective-permute-start.2 = (bf16[8,4096]{1,0:T(8,128)(2,1)}, bf16[8,4096]{1,0:T(8,128)(2,1)S(1)}, u32[]{:S(2)}, u32[]{:S(2)}) collective-permute-start(bf16[8,4096]{1,0:T(8,128)(2,1)} %param.9), channel_id=1, source_target_pairs={{0,192},{64,0},{128,64},{192,128},{1,193},{65,1},{129,65},{193,129... | collective-permute-start | bytes 196616 | tf_op jit(solution)/shard_map/ppermute | solution.py:89
  6.6 14.8 %collective-permute-start.1 = (bf16[8,4096]{1,0:T(8,128)(2,1)}, bf16[8,4096]{1,0:T(8,128)(2,1)S(1)}, u32[]{:S(2)}, u32[]{:S(2)}) collective-permute-start(bf16[8,4096]{1,0:T(8,128)(2,1)} %param.9), channel_id=1, source_target_pairs={{0,128},{64,192},{128,0},{192,64},{1,129},{65,193},{129,1},{193,65... | collective-permute-start | bytes 196616 | tf_op jit(solution)/shard_map/ppermute | solution.py:89
  7.3 14.2 %collective-permute-start = (bf16[8,4096]{1,0:T(8,128)(2,1)}, bf16[8,4096]{1,0:T(8,128)(2,1)S(1)}, u32[]{:S(2)}, u32[]{:S(2)}) collective-permute-start(bf16[8,4096]{1,0:T(8,128)(2,1)} %param.9), channel_id=1, source_target_pairs={{0,64},{64,128},{128,192},{192,0},{1,65},{65,129},{129,193},{193,1... | collective-permute-start | bytes 196616 | tf_op jit(solution)/shard_map/ppermute | solution.py:89
  8.2 31.5 %all-to-all-start = ((bf16[32,3,32,128]{3,2,1,0:T(8,128)(2,1)}), bf16[32,3,32,128]{3,2,1,0:T(8,128)(2,1)S(1)}, u32[]{:S(2)}, u32[]{:S(2)}) async-start(bf16[32,3,32,128]{3,2,1,0:T(8,128)(2,1)} %bitcast), calls=%async_computation | async-start | bytes 1572864 | tf_op jit(solution)/shard_map/all_to_all | solution.py:102
  19.9 12.9 %copy-start.4 = (bf16[4096,256]{1,0:T(8,128)(2,1)S(1)}, bf16[4096,256]{1,0:T(8,128)(2,1)}, u32[]{:S(2)}) copy-start(bf16[4096,256]{1,0:T(8,128)(2,1)} %param.16) | copy-start | bytes 6291460
  19.9 22.6 %collective-permute-start.8 = (bf16[4096,256]{1,0:T(8,128)(2,1)}, bf16[4096,256]{1,0:T(8,128)(2,1)}, u32[]{:S(2)}, u32[]{:S(2)}) collective-permute-start(bf16[4096,256]{1,0:T(8,128)(2,1)} %bitcast.59), channel_id=1, source_target_pairs={{0,32},{32,0},{1,33},{33,1},{2,34},{34,2},{3,35},{35,3},{4,36},{36... | collective-permute-start | bytes 6291464 | tf_op jit(solution)/shard_map/ppermute | solution.py:89
  20.0 25.0 %collective-permute-start.9 = (bf16[4096,256]{1,0:T(8,128)(2,1)}, bf16[4096,256]{1,0:T(8,128)(2,1)}, u32[]{:S(2)}, u32[]{:S(2)}) collective-permute-start(bf16[4096,256]{1,0:T(8,128)(2,1)} %bitcast.61), channel_id=1, source_target_pairs={{0,32},{32,0},{1,33},{33,1},{2,34},{34,2},{3,35},{35,3},{4,36},{36... | collective-permute-start | bytes 6291464 | tf_op jit(solution)/shard_map/ppermute | solution.py:89
  21.4 25.7 %collective-permute-start.10 = (bf16[256,4096]{1,0:T(8,128)(2,1)}, bf16[256,4096]{1,0:T(8,128)(2,1)}, u32[]{:S(2)}, u32[]{:S(2)}) collective-permute-start(bf16[256,4096]{1,0:T(8,128)(2,1)} %bitcast.63), channel_id=1, source_target_pairs={{0,32},{32,0},{1,33},{33,1},{2,34},{34,2},{3,35},{35,3},{4,36},{36... | collective-permute-start | bytes 6291464 | tf_op jit(solution)/shard_map/ppermute | solution.py:89
  22.3 8.4 %collective-permute-start.3 = (bf16[32,4096]{1,0:T(8,128)(2,1)S(1)}, bf16[32,4096]{1,0:T(8,128)(2,1)S(1)}, u32[]{:S(2)}, u32[]{:S(2)}) collective-permute-start(bf16[32,4096]{1,0:T(8,128)(2,1)S(1)} %pad_maximum_fusion.3), channel_id=1, source_target_pairs={{0,32},{32,0},{1,33},{33,1},{2,34},{34,2},{3,35},{35,3},{4,36},{36... | collective-permute-start | bytes 786440 | tf_op jit(solution)/shard_map/ppermute | solution.py:89
  40.1 17.7 %collective-permute-start.12 = (bf16[96,4096]{1,0:T(8,128)(2,1)S(1)}, bf16[96,4096]{1,0:T(8,128)(2,1)S(1)}, u32[]{:S(2)}, u32[]{:S(2)}) collective-permute-start(bf16[96,4096]{1,0:T(8,128)(2,1)S(1)} %bitcast.65), channel_id=1, source_target_pairs={{0,192},{64,0},{128,64},{192,128},{1,193},{65,1},{129,65},{193,129... | collective-permute-start | bytes 2359304 | tf_op jit(solution)/shard_map/ppermute | solution.py:89
  42.5 17.7 %collective-permute-start.11 = (bf16[96,4096]{1,0:T(8,128)(2,1)S(1)}, bf16[96,4096]{1,0:T(8,128)(2,1)S(1)}, u32[]{:S(2)}, u32[]{:S(2)}) collective-permute-start(bf16[96,4096]{1,0:T(8,128)(2,1)S(1)} %bitcast.66), channel_id=1, source_target_pairs={{0,64},{64,128},{128,192},{192,0},{1,65},{65,129},{129,193},{193,1... | collective-permute-start | bytes 2359304 | tf_op jit(solution)/shard_map/ppermute | solution.py:89
  57.8 15.9 %collective-permute-start.16 = (bf16[48,4096]{1,0:T(8,128)(2,1)S(1)}, bf16[48,4096]{1,0:T(8,128)(2,1)S(1)}, u32[]{:S(2)}, u32[]{:S(2)}) collective-permute-start(bf16[48,4096]{1,0:T(8,128)(2,1)S(1)} %slice.57), channel_id=1, source_target_pairs={{0,192},{64,0},{128,64},{192,128},{1,193},{65,1},{129,65},{193,129... | collective-permute-start | bytes 1179656 | tf_op jit(solution)/shard_map/ppermute | solution.py:89
  60.2 13.5 %collective-permute-start.15 = (bf16[48,4096]{1,0:T(8,128)(2,1)S(1)}, bf16[48,4096]{1,0:T(8,128)(2,1)S(1)}, u32[]{:S(2)}, u32[]{:S(2)}) collective-permute-start(bf16[48,4096]{1,0:T(8,128)(2,1)S(1)} %slice.56), channel_id=1, source_target_pairs={{0,64},{64,128},{128,192},{192,0},{1,65},{65,129},{129,193},{193,1... | collective-permute-start | bytes 1179656 | tf_op jit(solution)/shard_map/ppermute | solution.py:89
  63.7 34.1 %collective-permute-start.13 = (bf16[96,4096]{1,0:T(8,128)(2,1)S(1)}, bf16[96,4096]{1,0:T(8,128)(2,1)S(1)}, u32[]{:S(2)}, u32[]{:S(2)}) collective-permute-start(bf16[96,4096]{1,0:T(8,128)(2,1)S(1)} %get-tuple-element.21), channel_id=1, source_target_pairs={{0,192},{64,0},{128,64},{192,128},{1,193},{65,1},{129,65},{193,129... | collective-permute-start | bytes 2359304 | tf_op jit(solution)/shard_map/ppermute | solution.py:89
  67.0 34.2 %collective-permute-start.14 = (bf16[96,4096]{1,0:T(8,128)(2,1)S(1)}, bf16[96,4096]{1,0:T(8,128)(2,1)S(1)}, u32[]{:S(2)}, u32[]{:S(2)}) collective-permute-start(bf16[96,4096]{1,0:T(8,128)(2,1)S(1)} %get-tuple-element.22), channel_id=1, source_target_pairs={{0,64},{64,128},{128,192},{192,0},{1,65},{65,129},{129,193},{193,1... | collective-permute-start | bytes 2359304 | tf_op jit(solution)/shard_map/ppermute | solution.py:89
  76.1 25.1 %collective-permute-start.17 = (bf16[96,4096]{1,0:T(8,128)(2,1)S(1)}, bf16[96,4096]{1,0:T(8,128)(2,1)S(1)}, u32[]{:S(2)}, u32[]{:S(2)}) collective-permute-start(bf16[96,4096]{1,0:T(8,128)(2,1)S(1)} %convolution_convert_fusion.1), channel_id=1, source_target_pairs={{0,128},{64,192},{128,0},{192,64},{1,129},{65,193},{129,1},{193,65... | collective-permute-start | bytes 2359304 | tf_op jit(solution)/shard_map/ppermute | solution.py:89
  77.2 25.3 %copy-start.3 = (f32[64,4096]{1,0:T(8,128)}, f32[64,4096]{1,0:T(8,128)S(1)}, u32[]{:S(2)}) copy-start(f32[64,4096]{1,0:T(8,128)S(1)} %fusion.10) | copy-start | bytes 3145732
  77.2 39.3 %collective-permute-start.4 = (bf16[32,4096]{1,0:T(8,128)(2,1)S(1)}, bf16[32,4096]{1,0:T(8,128)(2,1)S(1)}, u32[]{:S(2)}, u32[]{:S(2)}) collective-permute-start(bf16[32,4096]{1,0:T(8,128)(2,1)S(1)} %slice.67), channel_id=1, source_target_pairs={{0,32},{32,0},{1,33},{33,1},{2,34},{34,2},{3,35},{35,3},{4,36},{36... | collective-permute-start | bytes 786440 | tf_op jit(solution)/shard_map/ppermute | solution.py:89
  102.5 31.1 %copy-start.1 = (f32[8,8]{1,0:T(8,128)S(1)}, f32[8,8]{1,0:T(8,128)}, u32[]{:S(2)}) copy-start(f32[8,8]{1,0:T(8,128)} %gates_ref.1) | copy-start | bytes 772
  103.6 30.1 %all-to-all-start.1 = ((bf16[32,3,32,128]{3,2,1,0:T(8,128)(2,1)}), bf16[32,3,32,128]{3,2,1,0:T(8,128)(2,1)S(1)}, u32[]{:S(2)}, u32[]{:S(2)}) async-start(bf16[32,3,32,128]{3,2,1,0:T(8,128)(2,1)} %bitcast.58), calls=%async_computation.1 | async-start | bytes 1572864 | tf_op jit(solution)/shard_map/all_to_all | solution.py:102
  117.6 4.3 %collective-permute-start.5 = (bf16[8,4096]{1,0:T(8,128)(2,1)S(1)}, bf16[8,4096]{1,0:T(8,128)(2,1)S(1)}, u32[]{:S(2)}, u32[]{:S(2)}) collective-permute-start(bf16[8,4096]{1,0:T(8,128)(2,1)S(1)} %get-tuple-element.23), channel_id=1, source_target_pairs={{0,192},{64,0},{128,64},{192,128},{1,193},{65,1},{129,65},{193,129... | collective-permute-start | bytes 196616 | tf_op jit(solution)/shard_map/ppermute | solution.py:89
  117.7 5.6 %collective-permute-start.7 = (bf16[8,4096]{1,0:T(8,128)(2,1)S(1)}, bf16[8,4096]{1,0:T(8,128)(2,1)S(1)}, u32[]{:S(2)}, u32[]{:S(2)}) collective-permute-start(bf16[8,4096]{1,0:T(8,128)(2,1)S(1)} %get-tuple-element.24), channel_id=1, source_target_pairs={{0,64},{64,128},{128,192},{192,0},{1,65},{65,129},{129,193},{193,1... | collective-permute-start | bytes 196616 | tf_op jit(solution)/shard_map/ppermute | solution.py:89
  119.8 5.8 %collective-permute-start.6 = (bf16[8,4096]{1,0:T(8,128)(2,1)S(1)}, bf16[8,4096]{1,0:T(8,128)(2,1)S(1)}, u32[]{:S(2)}, u32[]{:S(2)}) collective-permute-start(bf16[8,4096]{1,0:T(8,128)(2,1)S(1)} %get-tuple-element.25), channel_id=1, source_target_pairs={{0,128},{64,192},{128,0},{192,64},{1,129},{65,193},{129,1},{193,65... | collective-permute-start | bytes 196616 | tf_op jit(solution)/shard_map/ppermute | solution.py:89
  (3 other events, 7.8 us)
where the time goes:
time: 138 us; the launch traced here: 135 us
  waiting for transfers between devices  65.2 us (47%)
  starting transfers between devices  42 us (30%)
  matrix products  11 us (8%)
  other arithmetic  8.64 us (6%)
  local copies, waits for them, and re-layouts  5.22 us (4%)
  Pallas kernels  2.63 us (2%)
    ppermute x18, waiting for transfers between devices, shift(): return lax.ppermute(value, axis, [(i, (i + by) % n) for i in range(n)])  50.7 us
    all_to_all x2, starting transfers between devices, exchange(): lax.all_to_all(rows.reshape(split), ('x', 'z'), split_axis=0, concat_axis...  24.5 us
    ppermute x18, starting transfers between devices, shift(): return lax.ppermute(value, axis, [(i, (i + by) % n) for i in range(n)])  17.5 us
    all_to_all x2, waiting for transfers between devices, exchange(): lax.all_to_all(rows.reshape(split), ('x', 'z'), split_axis=0, concat_axis...  14.5 us
    unnamed x25, local copies, waits for them, and re-layouts  4.88 us
    concatenate x2, other arithmetic, layer(): jnp.concatenate(pair, axis=1)  4.56 us
    dot_general x4, matrix products, hidden_of(): gate = jnp.dot(rows, gate_w, preferred_element_type=jnp.float32)  4.52 us
    dot_general x4, matrix products, down(): return jnp.dot(hidden, down_w, preferred_element_type=jnp.float32)  3.5 us
  transfers between devices with their start and end apart: 20, of which 10 were waited for; matrix products, arithmetic and copies ran while one was open for 17% of the time, Pallas kernels for 0%

commit v1 on v0

--- a/solution.py
+++ b/solution.py
@@ -6,7 +6,6 @@
 from jax.sharding import Mesh, PartitionSpec as P
 
 CAP = 3
-PARTS = 1
 LANES = 128
 SMALL = pltpu.CompilerParams(vmem_limit_bytes=6 * 2**20)
 
@@ -50,28 +49,24 @@
     )(ids, rows3)
 
 
-def combine_rows(slots, gates, shared3, *returned):
+def combine_rows(slots, gates, shared3, returned):
     count, picks = slots.shape
-    folds = shared3.shape[1] // len(returned)
 
-    def kernel(slot_ref, gates_ref, shared_ref, *refs):
-        out_ref = refs[-1]
-        for index, ret_ref in enumerate(refs[:-1]):
-            part = slice(index * folds, (index + 1) * folds)
-            for r in range(count):
-                total = shared_ref[r, part]
-                for k in range(picks):
-                    total = total + gates_ref[r, k] * ret_ref[slot_ref[r, k]].astype(jnp.float32)
-                out_ref[r, part] = total.astype(out_ref.dtype)
+    def kernel(slot_ref, gates_ref, shared_ref, ret_ref, out_ref):
+        for r in range(count):
+            total = shared_ref[r]
+            for k in range(picks):
+                total = total + gates_ref[r, k] * ret_ref[slot_ref[r, k]].astype(jnp.float32)
+            out_ref[r] = total.astype(out_ref.dtype)
 
     return pl.pallas_call(
         kernel,
         out_shape=jax.ShapeDtypeStruct(shared3.shape, jnp.bfloat16),
-        in_specs=[in_smem(), in_smem(), in_vmem()] + [in_vmem() for _ in returned],
+        in_specs=[in_smem(), in_smem(), in_vmem(), in_vmem()],
         out_specs=in_vmem(),
         compiler_params=SMALL,
         name="combine_rows",
-    )(slots, gates, shared3, *returned)
+    )(slots, gates, shared3, returned)
 
 
 def hidden_of(rows, gate_w, up_w):
@@ -108,11 +103,7 @@
     own_w = (w_gate[0], w_up[0], w_down[0])
     other_w = [shift(w, "core", 1) for w in own_w]
     gate_w, up_w = (jnp.concatenate(pair, axis=1) for pair in zip(own_w[:2], other_w[:2]))
-    step = width // PARTS
-    down_w = [
-        jnp.concatenate([w[:, part * step : (part + 1) * step] for w in (own_w[2], other_w[2])], axis=0)
-        for part in range(PARTS)
-    ]
+    down_w = jnp.concatenate([own_w[2], other_w[2]], axis=0)
 
     arrived = exchange(packed, folds)
 
@@ -127,29 +118,29 @@
         back = shift(shared_part[by].astype(jnp.bfloat16), "y", planes - by)
         shared = shared + back.astype(jnp.float32)
 
-    gate_w, up_w, *down_w = lax.optimization_barrier((gate_w, up_w, *down_w))
+    gate_w, up_w, down_w = lax.optimization_barrier((gate_w, up_w, down_w))
 
     mine = arrived.reshape(slots, width)
     left, right = shift(mine, "y", 1), shift(mine, "y", planes - 1)
     far = [shift(left[:half], "y", 1), shift(right[half:], "y", planes - 1)]
     far = jnp.concatenate(far, axis=0)
 
-    own_hidden = hidden_of(mine, gate_w, up_w)
-    total = [down(own_hidden, w) for w in down_w]
-    near_hidden = hidden_of(jnp.concatenate([left, right], axis=0), gate_w, up_w)
-    near = [down(near_hidden, w).astype(jnp.bfloat16) for w in down_w]
-    far_hidden = hidden_of(far, gate_w, up_w)
-    far = [down(far_hidden, w).astype(jnp.bfloat16) for w in down_w]
+    total = down(hidden_of(mine, gate_w, up_w), down_w)
+    near = hidden_of(jnp.concatenate([left[:half], right[half:], left[half:], right[:half]], axis=0), gate_w, up_w)
+    free = down(near[:slots], down_w).astype(jnp.bfloat16)
+    held = down(near[slots:], down_w)
+    free = shift(free[half:], "y", 1), shift(free[:half], "y", planes - 1)
+    far = down(hidden_of(far, gate_w, up_w), down_w).astype(jnp.bfloat16)
+    far = shift(far[:half], "y", 1), shift(far[half:], "y", planes - 1)
+    upper = (held[half:] + far[0].astype(jnp.float32)).astype(jnp.bfloat16)
+    lower = (held[:half] + far[1].astype(jnp.float32)).astype(jnp.bfloat16)
+    held = shift(upper, "y", 1), shift(lower, "y", planes - 1)
+    back = (held[0], free[1]), (free[0], held[1])
+    back = [sum(value.astype(jnp.float32) for value in values) for values in back]
+    total = total + jnp.concatenate(back, axis=0)
+    returned = exchange(total.astype(jnp.bfloat16), folds)
 
-    returned = []
-    for part in range(PARTS):
-        back = [shift(near[part][:slots], "y", planes - 1), shift(near[part][slots:], "y", 1)]
-        back.append(shift(far[part], "y", 2))
-        for value in back:
-            total[part] = total[part] + value.astype(jnp.float32)
-        returned.append(exchange(total[part].astype(jnp.bfloat16), folds // PARTS))
-
-    mixed = combine_rows(places, gates, shared.reshape(own, folds, LANES), *returned)
+    mixed = combine_rows(places, gates, shared.reshape(own, folds, LANES), returned)
     return mixed.reshape(own, width)
 
 

time: 138 us -> 136 us (0.986)
  the two profiles are of different devices: /device:TPU:2 before, /device:TPU:56 now
where the time goes in v1:
time: 136 us; the launch traced here: 135 us
  waiting for transfers between devices  63.9 us (47%)
  starting transfers between devices  41.2 us (30%)
  matrix products  12.1 us (9%)
  other arithmetic  8.95 us (7%)
  local copies, waits for them, and re-layouts  6.26 us (5%)
  Pallas kernels  2.69 us (2%)
    ppermute x21, waiting for transfers between devices, shift(): return lax.ppermute(value, axis, [(i, (i + by) % n) for i in range(n)])  40 us
    all_to_all x2, waiting for transfers between devices, exchange(): lax.all_to_all(rows.reshape(split), ('x', 'z'), split_axis=0, concat_axis...  23.9 us
    all_to_all x2, starting transfers between devices, exchange(): lax.all_to_all(rows.reshape(split), ('x', 'z'), split_axis=0, concat_axis...  21.8 us
    ppermute x21, starting transfers between devices, shift(): return lax.ppermute(value, axis, [(i, (i + by) % n) for i in range(n)])  19.5 us
    unnamed x22, local copies, waits for them, and re-layouts  4.92 us
    dot_general x5, matrix products, down(): return jnp.dot(hidden, down_w, preferred_element_type=jnp.float32)  4.69 us
    concatenate x2, other arithmetic, layer(): jnp.concatenate(pair, axis=1)  4.57 us
    dot_general x4, matrix products, hidden_of(): gate = jnp.dot(rows, gate_w, preferred_element_type=jnp.float32)  4.5 us
  transfers between devices with their start and end apart: 23, of which 14 were waited for; matrix products, arithmetic and copies ran while one was open for 18% of the time, Pallas kernels for 0%

profile of v1, /device:TPU:56, one launch (start us, length us, event | category | flops | bytes accessed | tf_op | source)
XLA Modules:
  0.0 135.5 jit_solution(18378392492264066440)
XLA Ops:
  1.7 1.9 %pack_rows.1 = (bf16[96,32,128]{2,1,0:T(8,128)(2,1)}, s32[8,8]{1,0:T(8,128)S(1)}) custom-call(s32[8,8]{1,0:T(8,128)S(1)} %copy-done.2, bf16[8,32,128]{2,1,0:T(8,128)(2,1)S(1)} %bitcast.51), custom_call_target="tpu_custom_call" | custom-call | tf_op jit(solution)/shard_map/pack_rows/pallas_call | solution.py:38
  3.9 2.6 %collective-permute-start.1 = (bf16[8,4096]{1,0:T(8,128)(2,1)}, bf16[8,4096]{1,0:T(8,128)(2,1)S(1)}, u32[]{:S(2)}, u32[]{:S(2)}) collective-permute-start(bf16[8,4096]{1,0:T(8,128)(2,1)} %param.9), channel_id=1, source_target_pairs={{0,128},{64,192},{128,0},{192,64},{1,129},{65,193},{129,1},{193,65... | collective-permute-start | bytes 196616 | tf_op jit(solution)/shard_map/ppermute | solution.py:84
  7.0 11.2 %all-to-all-start = ((bf16[32,3,32,128]{3,2,1,0:T(8,128)(2,1)}), bf16[32,3,32,128]{3,2,1,0:T(8,128)(2,1)S(1)}, u32[]{:S(2)}, u32[]{:S(2)}) async-start(bf16[32,3,32,128]{3,2,1,0:T(8,128)(2,1)} %bitcast), calls=%async_computation | async-start | bytes 1572864 | tf_op jit(solution)/shard_map/all_to_all | solution.py:97
  20.7 3.3 %collective-permute-done.3 = bf16[32,4096]{1,0:T(8,128)(2,1)S(1)} collective-permute-done((bf16[32,4096]{1,0:T(8,128)(2,1)S(1)}, bf16[32,4096]{1,0:T(8,128)(2,1)S(1)}, u32[]{:S(2)}, u32[]{:S(2)}) %collective-permute-start.3) | collective-permute-done | bytes 262176 | tf_op jit(solution)/shard_map/ppermute | solution.py:84
  24.0 2.1 %fusion.22 = f32[64,256]{1,0:T(8,128)S(1)} fusion(bf16[64,4096]{1,0:T(8,128)(2,1)S(1)} %constant_dynamic-update-slice_fusion, bf16[4096,256]{1,0:T(8,128)(2,1)} %param.15), kind=kOutput, calls=%fused_computation.52 | convolution fusion | flops 134217728 | bytes 2686976 | tf_op jit(solution)/shard_map/dot_general | solution.py:73
  26.5 1.4 %fusion.23 = f32[64,4096]{1,0:T(8,128)} fusion(bf16[64,256]{1,0:T(8,128)(2,1)S(1)} %multiply_convert_fusion.2, bf16[256,4096]{1,0:T(8,128)(2,1)S(1)} %copy-done), kind=kOutput, calls=%fused_computation.53 | convolution fusion | flops 134217728 | bytes 3178496 | tf_op jit(solution)/shard_map/dot_general | solution.py:79
  29.3 12.1 %all-to-all-done = bf16[32,3,32,128]{3,2,1,0:T(8,128)(2,1)S(1)} async-done(((bf16[32,3,32,128]{3,2,1,0:T(8,128)(2,1)}), bf16[32,3,32,128]{3,2,1,0:T(8,128)(2,1)S(1)}, u32[]{:S(2)}, u32[]{:S(2)}) %all-to-all-start) | async-done | bytes 786464 | tf_op jit(solution)/shard_map/all_to_all | solution.py:97
  41.7 3.3 %collective-permute-start.11 = (bf16[96,4096]{1,0:T(8,128)(2,1)S(1)}, bf16[96,4096]{1,0:T(8,128)(2,1)S(1)}, u32[]{:S(2)}, u32[]{:S(2)}) collective-permute-start(bf16[96,4096]{1,0:T(8,128)(2,1)S(1)} %bitcast.63), channel_id=1, source_target_pairs={{0,64},{64,128},{128,192},{192,0},{1,65},{65,129},{129,193},{193,1... | collective-permute-start | bytes 2359304 | tf_op jit(solution)/shard_map/ppermute | solution.py:84
  45.1 2.5 %pad_maximum_fusion = bf16[4096,512]{1,0:T(8,128)(2,1)S(1)} fusion(bf16[4096,256]{1,0:T(8,128)(2,1)} %collective-permute-done.8, bf16[4096,256]{1,0:T(8,128)(2,1)} %bitcast.58), kind=kLoop, calls=%fused_computation.2 | loop fusion | flops 8388608 | bytes 8388608 | tf_op jit(solution)/shard_map/concatenate | solution.py:105
  47.6 2.0 %pad_maximum_fusion.1 = bf16[4096,512]{1,0:T(8,128)(2,1)S(1)} fusion(bf16[4096,256]{1,0:T(8,128)(2,1)} %collective-permute-done.9, bf16[4096,256]{1,0:T(8,128)(2,1)S(1)} %bitcast.60), kind=kLoop, calls=%fused_computation.3 | loop fusion | flops 8388608 | bytes 8388608 | tf_op jit(solution)/shard_map/concatenate | solution.py:105
  49.8 2.1 %pad_maximum_fusion.2 = bf16[512,4096]{1,0:T(8,128)(2,1)S(1)} fusion(bf16[256,4096]{1,0:T(8,128)(2,1)} %collective-permute-done.10, bf16[256,4096]{1,0:T(8,128)(2,1)S(1)} %bitcast.62), kind=kLoop, calls=%fused_computation.4 | loop fusion | flops 8388608 | bytes 8388608 | tf_op jit(solution)/shard_map/concatenate | solution.py:106
  51.9 7.9 %collective-permute-done.11 = bf16[96,4096]{1,0:T(8,128)(2,1)S(1)} collective-permute-done((bf16[96,4096]{1,0:T(8,128)(2,1)S(1)}, bf16[96,4096]{1,0:T(8,128)(2,1)S(1)}, u32[]{:S(2)}, u32[]{:S(2)}) %collective-permute-start.11) | collective-permute-done | bytes 786464 | tf_op jit(solution)/shard_map/ppermute | solution.py:84
  59.8 3.8 %collective-permute-start.13 = (bf16[48,4096]{1,0:T(8,128)(2,1)S(1)}, bf16[48,4096]{1,0:T(8,128)(2,1)S(1)}, u32[]{:S(2)}, u32[]{:S(2)}) collective-permute-start(bf16[48,4096]{1,0:T(8,128)(2,1)S(1)} %get-tuple-element.27), channel_id=1, source_target_pairs={{0,64},{64,128},{128,192},{192,0},{1,65},{65,129},{129,193},{193,1... | collective-permute-start | bytes 1179656 | tf_op jit(solution)/shard_map/ppermute | solution.py:84
  66.7 2.3 %collective-permute-done.13 = bf16[48,4096]{1,0:T(8,128)(2,1)S(1)} collective-permute-done((bf16[48,4096]{1,0:T(8,128)(2,1)S(1)}, bf16[48,4096]{1,0:T(8,128)(2,1)S(1)}, u32[]{:S(2)}, u32[]{:S(2)}) %collective-permute-start.13) | collective-permute-done | bytes 393248 | tf_op jit(solution)/shard_map/ppermute | solution.py:84
  69.1 3.8 %collective-permute-done.14 = bf16[48,4096]{1,0:T(8,128)(2,1)S(1)} collective-permute-done((bf16[48,4096]{1,0:T(8,128)(2,1)S(1)}, bf16[48,4096]{1,0:T(8,128)(2,1)S(1)}, u32[]{:S(2)}, u32[]{:S(2)}) %collective-permute-start.14) | collective-permute-done | bytes 393248 | tf_op jit(solution)/shard_map/ppermute | solution.py:84
  75.5 2.0 %collective-permute-start.19 = (bf16[48,4096]{1,0:T(8,128)(2,1)S(1)}, bf16[48,4096]{1,0:T(8,128)(2,1)S(1)}, u32[]{:S(2)}, u32[]{:S(2)}) collective-permute-start(bf16[48,4096]{1,0:T(8,128)(2,1)S(1)} %get-tuple-element.24), channel_id=1, source_target_pairs={{0,192},{64,0},{128,64},{192,128},{1,193},{65,1},{129,65},{193,129... | collective-permute-start | bytes 1179656 | tf_op jit(solution)/shard_map/ppermute | solution.py:84
  78.5 6.3 %collective-permute-done.15 = bf16[48,4096]{1,0:T(8,128)(2,1)S(1)} collective-permute-done((bf16[48,4096]{1,0:T(8,128)(2,1)S(1)}, bf16[48,4096]{1,0:T(8,128)(2,1)S(1)}, u32[]{:S(2)}, u32[]{:S(2)}) %collective-permute-start.15) | collective-permute-done | bytes 393248 | tf_op jit(solution)/shard_map/ppermute | solution.py:84
  84.7 4.1 %collective-permute-done.19 = bf16[48,4096]{1,0:T(8,128)(2,1)S(1)} collective-permute-done((bf16[48,4096]{1,0:T(8,128)(2,1)S(1)}, bf16[48,4096]{1,0:T(8,128)(2,1)S(1)}, u32[]{:S(2)}, u32[]{:S(2)}) %collective-permute-start.19) | collective-permute-done | bytes 393248 | tf_op jit(solution)/shard_map/ppermute | solution.py:84
  92.6 3.4 %collective-permute-done.17 = bf16[48,4096]{1,0:T(8,128)(2,1)S(1)} collective-permute-done((bf16[48,4096]{1,0:T(8,128)(2,1)S(1)}, bf16[48,4096]{1,0:T(8,128)(2,1)S(1)}, u32[]{:S(2)}, u32[]{:S(2)}) %collective-permute-start.17) | collective-permute-done | bytes 393248 | tf_op jit(solution)/shard_map/ppermute | solution.py:84
  96.9 4.1 %collective-permute-done.18 = bf16[48,4096]{1,0:T(8,128)(2,1)S(1)} collective-permute-done((bf16[48,4096]{1,0:T(8,128)(2,1)S(1)}, bf16[48,4096]{1,0:T(8,128)(2,1)S(1)}, u32[]{:S(2)}, u32[]{:S(2)}) %collective-permute-start.18) | collective-permute-done | bytes 393248 | tf_op jit(solution)/shard_map/ppermute | solution.py:84
  103.0 10.6 %all-to-all-start.1 = ((bf16[32,3,32,128]{3,2,1,0:T(8,128)(2,1)}), bf16[32,3,32,128]{3,2,1,0:T(8,128)(2,1)S(1)}, u32[]{:S(2)}, u32[]{:S(2)}) async-start(bf16[32,3,32,128]{3,2,1,0:T(8,128)(2,1)} %bitcast.56), calls=%async_computation.1 | async-start | bytes 1572864 | tf_op jit(solution)/shard_map/all_to_all | solution.py:97
  115.2 2.7 %collective-permute-start.6 = (bf16[8,4096]{1,0:T(8,128)(2,1)S(1)}, bf16[8,4096]{1,0:T(8,128)(2,1)S(1)}, u32[]{:S(2)}, u32[]{:S(2)}) collective-permute-start(bf16[8,4096]{1,0:T(8,128)(2,1)S(1)} %get-tuple-element.33), channel_id=1, source_target_pairs={{0,128},{64,192},{128,0},{192,64},{1,129},{65,193},{129,1},{193,65... | collective-permute-start | bytes 196616 | tf_op jit(solution)/shard_map/ppermute | solution.py:84
  118.2 2.1 %collective-permute-done.5 = bf16[8,4096]{1,0:T(8,128)(2,1)S(1)} collective-permute-done((bf16[8,4096]{1,0:T(8,128)(2,1)S(1)}, bf16[8,4096]{1,0:T(8,128)(2,1)S(1)}, u32[]{:S(2)}, u32[]{:S(2)}) %collective-permute-start.5) | collective-permute-done | bytes 65568 | tf_op jit(solution)/shard_map/ppermute | solution.py:84
  122.3 11.8 %all-to-all-done.1 = bf16[32,3,32,128]{3,2,1,0:T(8,128)(2,1)S(1)} async-done(((bf16[32,3,32,128]{3,2,1,0:T(8,128)(2,1)}), bf16[32,3,32,128]{3,2,1,0:T(8,128)(2,1)S(1)}, u32[]{:S(2)}, u32[]{:S(2)}) %all-to-all-start.1) | async-done | bytes 786464 | tf_op jit(solution)/shard_map/all_to_all | solution.py:97
  (76 shorter events, 25.8 us)
Async XLA Ops:
  3.6 15.6 %collective-permute-start = (bf16[8,4096]{1,0:T(8,128)(2,1)}, bf16[8,4096]{1,0:T(8,128)(2,1)S(1)}, u32[]{:S(2)}, u32[]{:S(2)}) collective-permute-start(bf16[8,4096]{1,0:T(8,128)(2,1)} %param.9), channel_id=1, source_target_pairs={{0,64},{64,128},{128,192},{192,0},{1,65},{65,129},{129,193},{193,1... | collective-permute-start | bytes 196616 | tf_op jit(solution)/shard_map/ppermute | solution.py:84
  3.9 15.3 %collective-permute-start.1 = (bf16[8,4096]{1,0:T(8,128)(2,1)}, bf16[8,4096]{1,0:T(8,128)(2,1)S(1)}, u32[]{:S(2)}, u32[]{:S(2)}) collective-permute-start(bf16[8,4096]{1,0:T(8,128)(2,1)} %param.9), channel_id=1, source_target_pairs={{0,128},{64,192},{128,0},{192,64},{1,129},{65,193},{129,1},{193,65... | collective-permute-start | bytes 196616 | tf_op jit(solution)/shard_map/ppermute | solution.py:84
  6.5 12.7 %collective-permute-start.2 = (bf16[8,4096]{1,0:T(8,128)(2,1)}, bf16[8,4096]{1,0:T(8,128)(2,1)S(1)}, u32[]{:S(2)}, u32[]{:S(2)}) collective-permute-start(bf16[8,4096]{1,0:T(8,128)(2,1)} %param.9), channel_id=1, source_target_pairs={{0,192},{64,0},{128,64},{192,128},{1,193},{65,1},{129,65},{193,129... | collective-permute-start | bytes 196616 | tf_op jit(solution)/shard_map/ppermute | solution.py:84
  6.5 38.5 %collective-permute-start.8 = (bf16[4096,256]{1,0:T(8,128)(2,1)}, bf16[4096,256]{1,0:T(8,128)(2,1)}, u32[]{:S(2)}, u32[]{:S(2)}) collective-permute-start(bf16[4096,256]{1,0:T(8,128)(2,1)} %bitcast.57), channel_id=1, source_target_pairs={{0,32},{32,0},{1,33},{33,1},{2,34},{34,2},{3,35},{35,3},{4,36},{36... | collective-permute-start | bytes 6291464 | tf_op jit(solution)/shard_map/ppermute | solution.py:84
  6.5 41.1 %collective-permute-start.9 = (bf16[4096,256]{1,0:T(8,128)(2,1)}, bf16[4096,256]{1,0:T(8,128)(2,1)}, u32[]{:S(2)}, u32[]{:S(2)}) collective-permute-start(bf16[4096,256]{1,0:T(8,128)(2,1)} %bitcast.59), channel_id=1, source_target_pairs={{0,32},{32,0},{1,33},{33,1},{2,34},{34,2},{3,35},{35,3},{4,36},{36... | collective-permute-start | bytes 6291464 | tf_op jit(solution)/shard_map/ppermute | solution.py:84
  7.0 34.4 %all-to-all-start = ((bf16[32,3,32,128]{3,2,1,0:T(8,128)(2,1)}), bf16[32,3,32,128]{3,2,1,0:T(8,128)(2,1)S(1)}, u32[]{:S(2)}, u32[]{:S(2)}) async-start(bf16[32,3,32,128]{3,2,1,0:T(8,128)(2,1)} %bitcast), calls=%async_computation | async-start | bytes 1572864 | tf_op jit(solution)/shard_map/all_to_all | solution.py:97
  19.2 30.4 %collective-permute-start.10 = (bf16[256,4096]{1,0:T(8,128)(2,1)}, bf16[256,4096]{1,0:T(8,128)(2,1)}, u32[]{:S(2)}, u32[]{:S(2)}) collective-permute-start(bf16[256,4096]{1,0:T(8,128)(2,1)} %bitcast.61), channel_id=1, source_target_pairs={{0,32},{32,0},{1,33},{33,1},{2,34},{34,2},{3,35},{35,3},{4,36},{36... | collective-permute-start | bytes 6291464 | tf_op jit(solution)/shard_map/ppermute | solution.py:84
  20.1 3.8 %collective-permute-start.3 = (bf16[32,4096]{1,0:T(8,128)(2,1)S(1)}, bf16[32,4096]{1,0:T(8,128)(2,1)S(1)}, u32[]{:S(2)}, u32[]{:S(2)}) collective-permute-start(bf16[32,4096]{1,0:T(8,128)(2,1)S(1)} %pad_maximum_fusion.8), channel_id=1, source_target_pairs={{0,32},{32,0},{1,33},{33,1},{2,34},{34,2},{3,35},{35,3},{4,36},{36... | collective-permute-start | bytes 786440 | tf_op jit(solution)/shard_map/ppermute | solution.py:84
  29.1 84.5 %collective-permute-start.4 = (bf16[32,4096]{1,0:T(8,128)(2,1)S(1)}, bf16[32,4096]{1,0:T(8,128)(2,1)S(1)}, u32[]{:S(2)}, u32[]{:S(2)}) collective-permute-start(bf16[32,4096]{1,0:T(8,128)(2,1)S(1)} %slice.119), channel_id=1, source_target_pairs={{0,32},{32,0},{1,33},{33,1},{2,34},{34,2},{3,35},{35,3},{4,36},{36... | collective-permute-start | bytes 786440 | tf_op jit(solution)/shard_map/ppermute | solution.py:84
  41.7 18.0 %collective-permute-start.11 = (bf16[96,4096]{1,0:T(8,128)(2,1)S(1)}, bf16[96,4096]{1,0:T(8,128)(2,1)S(1)}, u32[]{:S(2)}, u32[]{:S(2)}) collective-permute-start(bf16[96,4096]{1,0:T(8,128)(2,1)S(1)} %bitcast.63), channel_id=1, source_target_pairs={{0,64},{64,128},{128,192},{192,0},{1,65},{65,129},{129,193},{193,1... | collective-permute-start | bytes 2359304 | tf_op jit(solution)/shard_map/ppermute | solution.py:84
  45.1 18.6 %collective-permute-start.12 = (bf16[96,4096]{1,0:T(8,128)(2,1)S(1)}, bf16[96,4096]{1,0:T(8,128)(2,1)S(1)}, u32[]{:S(2)}, u32[]{:S(2)}) collective-permute-start(bf16[96,4096]{1,0:T(8,128)(2,1)S(1)} %bitcast.64), channel_id=1, source_target_pairs={{0,192},{64,0},{128,64},{192,128},{1,193},{65,1},{129,65},{193,129... | collective-permute-start | bytes 2359304 | tf_op jit(solution)/shard_map/ppermute | solution.py:84
  59.8 9.2 %collective-permute-start.13 = (bf16[48,4096]{1,0:T(8,128)(2,1)S(1)}, bf16[48,4096]{1,0:T(8,128)(2,1)S(1)}, u32[]{:S(2)}, u32[]{:S(2)}) collective-permute-start(bf16[48,4096]{1,0:T(8,128)(2,1)S(1)} %get-tuple-element.27), channel_id=1, source_target_pairs={{0,64},{64,128},{128,192},{192,0},{1,65},{65,129},{129,193},{193,1... | collective-permute-start | bytes 1179656 | tf_op jit(solution)/shard_map/ppermute | solution.py:84
  63.7 9.2 %collective-permute-start.14 = (bf16[48,4096]{1,0:T(8,128)(2,1)S(1)}, bf16[48,4096]{1,0:T(8,128)(2,1)S(1)}, u32[]{:S(2)}, u32[]{:S(2)}) collective-permute-start(bf16[48,4096]{1,0:T(8,128)(2,1)S(1)} %get-tuple-element.29), channel_id=1, source_target_pairs={{0,192},{64,0},{128,64},{192,128},{1,193},{65,1},{129,65},{193,129... | collective-permute-start | bytes 1179656 | tf_op jit(solution)/shard_map/ppermute | solution.py:84
  75.4 9.3 %collective-permute-start.15 = (bf16[48,4096]{1,0:T(8,128)(2,1)S(1)}, bf16[48,4096]{1,0:T(8,128)(2,1)S(1)}, u32[]{:S(2)}, u32[]{:S(2)}) collective-permute-start(bf16[48,4096]{1,0:T(8,128)(2,1)S(1)} %get-tuple-element.23), channel_id=1, source_target_pairs={{0,64},{64,128},{128,192},{192,0},{1,65},{65,129},{129,193},{193,1... | collective-permute-start | bytes 1179656 | tf_op jit(solution)/shard_map/ppermute | solution.py:84
  75.5 13.3 %collective-permute-start.19 = (bf16[48,4096]{1,0:T(8,128)(2,1)S(1)}, bf16[48,4096]{1,0:T(8,128)(2,1)S(1)}, u32[]{:S(2)}, u32[]{:S(2)}) collective-permute-start(bf16[48,4096]{1,0:T(8,128)(2,1)S(1)} %get-tuple-element.24), channel_id=1, source_target_pairs={{0,192},{64,0},{128,64},{192,128},{1,193},{65,1},{129,65},{193,129... | collective-permute-start | bytes 1179656 | tf_op jit(solution)/shard_map/ppermute | solution.py:84
  77.6 18.4 %collective-permute-start.17 = (bf16[48,4096]{1,0:T(8,128)(2,1)S(1)}, bf16[48,4096]{1,0:T(8,128)(2,1)S(1)}, u32[]{:S(2)}, u32[]{:S(2)}) collective-permute-start(bf16[48,4096]{1,0:T(8,128)(2,1)S(1)} %get-tuple-element.25), channel_id=1, source_target_pairs={{0,192},{64,0},{128,64},{192,128},{1,193},{65,1},{129,65},{193,129... | collective-permute-start | bytes 1179656 | tf_op jit(solution)/shard_map/ppermute | solution.py:84
  88.9 7.9 %collective-permute-start.16 = (bf16[48,4096]{1,0:T(8,128)(2,1)S(1)}, bf16[48,4096]{1,0:T(8,128)(2,1)S(1)}, u32[]{:S(2)}, u32[]{:S(2)}) collective-permute-start(bf16[48,4096]{1,0:T(8,128)(2,1)S(1)} %get-tuple-element.21), channel_id=1, source_target_pairs={{0,64},{64,128},{128,192},{192,0},{1,65},{65,129},{129,193},{193,1... | collective-permute-start | bytes 1179656 | tf_op jit(solution)/shard_map/ppermute | solution.py:84
  90.4 10.6 %collective-permute-start.18 = (bf16[48,4096]{1,0:T(8,128)(2,1)S(1)}, bf16[48,4096]{1,0:T(8,128)(2,1)S(1)}, u32[]{:S(2)}, u32[]{:S(2)}) collective-permute-start(bf16[48,4096]{1,0:T(8,128)(2,1)S(1)} %get-tuple-element.26), channel_id=1, source_target_pairs={{0,64},{64,128},{128,192},{192,0},{1,65},{65,129},{129,193},{193,1... | collective-permute-start | bytes 1179656 | tf_op jit(solution)/shard_map/ppermute | solution.py:84
  91.8 9.2 %collective-permute-start.20 = (bf16[48,4096]{1,0:T(8,128)(2,1)S(1)}, bf16[48,4096]{1,0:T(8,128)(2,1)S(1)}, u32[]{:S(2)}, u32[]{:S(2)}) collective-permute-start(bf16[48,4096]{1,0:T(8,128)(2,1)S(1)} %get-tuple-element.22), channel_id=1, source_target_pairs={{0,192},{64,0},{128,64},{192,128},{1,193},{65,1},{129,65},{193,129... | collective-permute-start | bytes 1179656 | tf_op jit(solution)/shard_map/ppermute | solution.py:84
  101.9 32.1 %copy-start.1 = (f32[8,8]{1,0:T(8,128)S(1)}, f32[8,8]{1,0:T(8,128)}, u32[]{:S(2)}) copy-start(f32[8,8]{1,0:T(8,128)} %gates_ref.1) | copy-start | bytes 772
  103.0 31.1 %all-to-all-start.1 = ((bf16[32,3,32,128]{3,2,1,0:T(8,128)(2,1)}), bf16[32,3,32,128]{3,2,1,0:T(8,128)(2,1)S(1)}, u32[]{:S(2)}, u32[]{:S(2)}) async-start(bf16[32,3,32,128]{3,2,1,0:T(8,128)(2,1)} %bitcast.56), calls=%async_computation.1 | async-start | bytes 1572864 | tf_op jit(solution)/shard_map/all_to_all | solution.py:97
  114.7 5.6 %collective-permute-start.5 = (bf16[8,4096]{1,0:T(8,128)(2,1)S(1)}, bf16[8,4096]{1,0:T(8,128)(2,1)S(1)}, u32[]{:S(2)}, u32[]{:S(2)}) collective-permute-start(bf16[8,4096]{1,0:T(8,128)(2,1)S(1)} %get-tuple-element.31), channel_id=1, source_target_pairs={{0,192},{64,0},{128,64},{192,128},{1,193},{65,1},{129,65},{193,129... | collective-permute-start | bytes 196616 | tf_op jit(solution)/shard_map/ppermute | solution.py:84
  115.2 5.8 %collective-permute-start.6 = (bf16[8,4096]{1,0:T(8,128)(2,1)S(1)}, bf16[8,4096]{1,0:T(8,128)(2,1)S(1)}, u32[]{:S(2)}, u32[]{:S(2)}) collective-permute-start(bf16[8,4096]{1,0:T(8,128)(2,1)S(1)} %get-tuple-element.33), channel_id=1, source_target_pairs={{0,128},{64,192},{128,0},{192,64},{1,129},{65,193},{129,1},{193,65... | collective-permute-start | bytes 196616 | tf_op jit(solution)/shard_map/ppermute | solution.py:84
  117.9 4.3 %collective-permute-start.7 = (bf16[8,4096]{1,0:T(8,128)(2,1)S(1)}, bf16[8,4096]{1,0:T(8,128)(2,1)S(1)}, u32[]{:S(2)}, u32[]{:S(2)}) collective-permute-start(bf16[8,4096]{1,0:T(8,128)(2,1)S(1)} %get-tuple-element.32), channel_id=1, source_target_pairs={{0,64},{64,128},{128,192},{192,0},{1,65},{65,129},{129,193},{193,1... | collective-permute-start | bytes 196616 | tf_op jit(solution)/shard_map/ppermute | solution.py:84
  (5 other events, 43.2 us)

commit v2 on v1

--- a/solution.py
+++ b/solution.py
@@ -18,7 +18,7 @@
     return pl.BlockSpec(memory_space=pltpu.VMEM)
 
 
-def pack_rows(ids, rows3, experts):
+def pack_rows(ids, rows3, experts, order):
     count, picks = ids.shape
 
     def kernel(ids_ref, rows_ref, out_ref, slot_ref, used_ref):
@@ -31,7 +31,7 @@
                 e = ids_ref[r, k]
                 n = used_ref[e]
                 used_ref[e] = n + 1
-                slot = e * CAP + n
+                slot = order(e) * CAP + n
                 slot_ref[r, k] = slot
                 out_ref[slot] = row
 
@@ -86,18 +86,21 @@
 
 def layer(tokens, ids, gates, w_gate, w_up, w_down, s_gate, s_up, s_down):
     experts = lax.axis_size(("x", "z"))
-    planes = lax.axis_size("y")
+    planes, columns = lax.axis_size("y"), lax.axis_size("x")
     own, width = tokens.shape
     folds = width // LANES
     slots = experts * CAP
     half = slots // 2
 
+    def by_z(e):
+        return lax.rem(e, experts // columns) * columns + lax.div(e, experts // columns)
+
     def exchange(rows, part):
         split = (experts, CAP, part, LANES)
-        arrived = lax.all_to_all(rows.reshape(split), ("x", "z"), split_axis=0, concat_axis=0, tiled=True)
+        arrived = lax.all_to_all(rows.reshape(split), ("z", "x"), split_axis=0, concat_axis=0, tiled=True)
         return arrived.reshape(slots, part, LANES)
 
-    packed, places = pack_rows(ids, tokens.reshape(own, folds, LANES), experts)
+    packed, places = pack_rows(ids, tokens.reshape(own, folds, LANES), experts, by_z)
     early, packed = lax.optimization_barrier((tokens, packed))
 
     own_w = (w_gate[0], w_up[0], w_down[0])

time: 136 us -> 134 us (0.985)
  the two profiles are of different devices: /device:TPU:56 before, /device:TPU:2 now
where the time goes in v2:
time: 134 us; the launch traced here: 132 us
  waiting for transfers between devices  53.6 us (40%)
  starting transfers between devices  48.2 us (36%)
  matrix products  12.1 us (9%)
  other arithmetic  8.95 us (7%)
  local copies, waits for them, and re-layouts  6.26 us (5%)
  Pallas kernels  2.82 us (2%)
    ppermute x21, waiting for transfers between devices, shift(): return lax.ppermute(value, axis, [(i, (i + by) % n) for i in range(n)])  34.1 us
    ppermute x21, starting transfers between devices, shift(): return lax.ppermute(value, axis, [(i, (i + by) % n) for i in range(n)])  28.1 us
    all_to_all x2, starting transfers between devices, exchange(): lax.all_to_all(rows.reshape(split), ('z', 'x'), split_axis=0, concat_axis...  20.2 us
    all_to_all x2, waiting for transfers between devices, exchange(): lax.all_to_all(rows.reshape(split), ('z', 'x'), split_axis=0, concat_axis...  19.5 us
    unnamed x22, local copies, waits for them, and re-layouts  4.92 us
    dot_general x5, matrix products, down(): return jnp.dot(hidden, down_w, preferred_element_type=jnp.float32)  4.69 us
    concatenate x2, other arithmetic, layer(): jnp.concatenate(pair, axis=1)  4.56 us
    dot_general x4, matrix products, hidden_of(): gate = jnp.dot(rows, gate_w, preferred_element_type=jnp.float32)  4.5 us
  transfers between devices with their start and end apart: 23, of which 13 were waited for; matrix products, arithmetic and copies ran while one was open for 19% of the time, Pallas kernels for 0%

profile of v2, /device:TPU:2, one launch (start us, length us, event | category | flops | bytes accessed | tf_op | source)
XLA Modules:
  0.0 132.4 jit_solution(6931999027367673660)
XLA Ops:
  1.7 2.0 %pack_rows.1 = (bf16[96,32,128]{2,1,0:T(8,128)(2,1)}, s32[8,8]{1,0:T(8,128)S(1)}) custom-call(s32[8,8]{1,0:T(8,128)S(1)} %copy-done.2, bf16[8,32,128]{2,1,0:T(8,128)(2,1)S(1)} %bitcast.51), custom_call_target="tpu_custom_call" | custom-call | tf_op jit(solution)/shard_map/pack_rows/pallas_call | solution.py:38
  5.4 2.9 %collective-permute-start.1 = (bf16[8,4096]{1,0:T(8,128)(2,1)}, bf16[8,4096]{1,0:T(8,128)(2,1)S(1)}, u32[]{:S(2)}, u32[]{:S(2)}) collective-permute-start(bf16[8,4096]{1,0:T(8,128)(2,1)} %param.9), channel_id=1, source_target_pairs={{0,128},{64,192},{128,0},{192,64},{1,129},{65,193},{129,1},{193,65... | collective-permute-start | bytes 196616 | tf_op jit(solution)/shard_map/ppermute | solution.py:84
  10.2 11.6 %all-to-all-start = ((bf16[32,3,32,128]{3,2,1,0:T(8,128)(2,1)}), bf16[32,3,32,128]{3,2,1,0:T(8,128)(2,1)S(1)}, u32[]{:S(2)}, u32[]{:S(2)}) async-start(bf16[32,3,32,128]{3,2,1,0:T(8,128)(2,1)} %bitcast), calls=%async_computation | async-start | bytes 1572864 | tf_op jit(solution)/shard_map/all_to_all | solution.py:100
  24.3 3.3 %collective-permute-done.3 = bf16[32,4096]{1,0:T(8,128)(2,1)S(1)} collective-permute-done((bf16[32,4096]{1,0:T(8,128)(2,1)S(1)}, bf16[32,4096]{1,0:T(8,128)(2,1)S(1)}, u32[]{:S(2)}, u32[]{:S(2)}) %collective-permute-start.3) | collective-permute-done | bytes 262176 | tf_op jit(solution)/shard_map/ppermute | solution.py:84
  27.6 2.1 %fusion.22 = f32[64,256]{1,0:T(8,128)S(1)} fusion(bf16[64,4096]{1,0:T(8,128)(2,1)S(1)} %constant_dynamic-update-slice_fusion, bf16[4096,256]{1,0:T(8,128)(2,1)} %param.15), kind=kOutput, calls=%fused_computation.52 | convolution fusion | flops 134217728 | bytes 2686976 | tf_op jit(solution)/shard_map/dot_general | solution.py:73
  32.8 11.5 %all-to-all-done = bf16[32,3,32,128]{3,2,1,0:T(8,128)(2,1)S(1)} async-done(((bf16[32,3,32,128]{3,2,1,0:T(8,128)(2,1)}), bf16[32,3,32,128]{3,2,1,0:T(8,128)(2,1)S(1)}, u32[]{:S(2)}, u32[]{:S(2)}) %all-to-all-start) | async-done | bytes 786464 | tf_op jit(solution)/shard_map/all_to_all | solution.py:100
  45.5 2.6 %collective-permute-start.12 = (bf16[96,4096]{1,0:T(8,128)(2,1)S(1)}, bf16[96,4096]{1,0:T(8,128)(2,1)S(1)}, u32[]{:S(2)}, u32[]{:S(2)}) collective-permute-start(bf16[96,4096]{1,0:T(8,128)(2,1)S(1)} %bitcast.64), channel_id=1, source_target_pairs={{0,192},{64,0},{128,64},{192,128},{1,193},{65,1},{129,65},{193,129... | collective-permute-start | bytes 2359304 | tf_op jit(solution)/shard_map/ppermute | solution.py:84
  48.0 2.5 %pad_maximum_fusion = bf16[4096,512]{1,0:T(8,128)(2,1)S(1)} fusion(bf16[4096,256]{1,0:T(8,128)(2,1)} %collective-permute-done.8, bf16[4096,256]{1,0:T(8,128)(2,1)} %bitcast.58), kind=kLoop, calls=%fused_computation.2 | loop fusion | flops 8388608 | bytes 8388608 | tf_op jit(solution)/shard_map/concatenate | solution.py:108
  50.6 2.0 %pad_maximum_fusion.1 = bf16[4096,512]{1,0:T(8,128)(2,1)S(1)} fusion(bf16[4096,256]{1,0:T(8,128)(2,1)} %collective-permute-done.9, bf16[4096,256]{1,0:T(8,128)(2,1)S(1)} %bitcast.60), kind=kLoop, calls=%fused_computation.3 | loop fusion | flops 8388608 | bytes 8388608 | tf_op jit(solution)/shard_map/concatenate | solution.py:108
  52.8 2.1 %pad_maximum_fusion.2 = bf16[512,4096]{1,0:T(8,128)(2,1)S(1)} fusion(bf16[256,4096]{1,0:T(8,128)(2,1)} %collective-permute-done.10, bf16[256,4096]{1,0:T(8,128)(2,1)S(1)} %bitcast.62), kind=kLoop, calls=%fused_computation.4 | loop fusion | flops 8388608 | bytes 8388608 | tf_op jit(solution)/shard_map/concatenate | solution.py:109
  54.9 8.8 %collective-permute-done.11 = bf16[96,4096]{1,0:T(8,128)(2,1)S(1)} collective-permute-done((bf16[96,4096]{1,0:T(8,128)(2,1)S(1)}, bf16[96,4096]{1,0:T(8,128)(2,1)S(1)}, u32[]{:S(2)}, u32[]{:S(2)}) %collective-permute-start.11) | collective-permute-done | bytes 786464 | tf_op jit(solution)/shard_map/ppermute | solution.py:84
  63.9 3.5 %collective-permute-start.14 = (bf16[48,4096]{1,0:T(8,128)(2,1)S(1)}, bf16[48,4096]{1,0:T(8,128)(2,1)S(1)}, u32[]{:S(2)}, u32[]{:S(2)}) collective-permute-start(bf16[48,4096]{1,0:T(8,128)(2,1)S(1)} %get-tuple-element.29), channel_id=1, source_target_pairs={{0,192},{64,0},{128,64},{192,128},{1,193},{65,1},{129,65},{193,129... | collective-permute-start | bytes 1179656 | tf_op jit(solution)/shard_map/ppermute | solution.py:84
  70.2 3.3 %collective-permute-done.13 = bf16[48,4096]{1,0:T(8,128)(2,1)S(1)} collective-permute-done((bf16[48,4096]{1,0:T(8,128)(2,1)S(1)}, bf16[48,4096]{1,0:T(8,128)(2,1)S(1)}, u32[]{:S(2)}, u32[]{:S(2)}) %collective-permute-start.13) | collective-permute-done | bytes 393248 | tf_op jit(solution)/shard_map/ppermute | solution.py:84
  76.1 3.3 %collective-permute-start.19 = (bf16[48,4096]{1,0:T(8,128)(2,1)S(1)}, bf16[48,4096]{1,0:T(8,128)(2,1)S(1)}, u32[]{:S(2)}, u32[]{:S(2)}) collective-permute-start(bf16[48,4096]{1,0:T(8,128)(2,1)S(1)} %get-tuple-element.24), channel_id=1, source_target_pairs={{0,192},{64,0},{128,64},{192,128},{1,193},{65,1},{129,65},{193,129... | collective-permute-start | bytes 1179656 | tf_op jit(solution)/shard_map/ppermute | solution.py:84
  79.4 2.0 %collective-permute-start.17 = (bf16[48,4096]{1,0:T(8,128)(2,1)S(1)}, bf16[48,4096]{1,0:T(8,128)(2,1)S(1)}, u32[]{:S(2)}, u32[]{:S(2)}) collective-permute-start(bf16[48,4096]{1,0:T(8,128)(2,1)S(1)} %get-tuple-element.25), channel_id=1, source_target_pairs={{0,192},{64,0},{128,64},{192,128},{1,193},{65,1},{129,65},{193,129... | collective-permute-start | bytes 1179656 | tf_op jit(solution)/shard_map/ppermute | solution.py:84
  82.2 3.3 %collective-permute-done.15 = bf16[48,4096]{1,0:T(8,128)(2,1)S(1)} collective-permute-done((bf16[48,4096]{1,0:T(8,128)(2,1)S(1)}, bf16[48,4096]{1,0:T(8,128)(2,1)S(1)}, u32[]{:S(2)}, u32[]{:S(2)}) %collective-permute-start.15) | collective-permute-done | bytes 393248 | tf_op jit(solution)/shard_map/ppermute | solution.py:84
  85.5 3.3 %collective-permute-done.19 = bf16[48,4096]{1,0:T(8,128)(2,1)S(1)} collective-permute-done((bf16[48,4096]{1,0:T(8,128)(2,1)S(1)}, bf16[48,4096]{1,0:T(8,128)(2,1)S(1)}, u32[]{:S(2)}, u32[]{:S(2)}) %collective-permute-start.19) | collective-permute-done | bytes 393248 | tf_op jit(solution)/shard_map/ppermute | solution.py:84
  89.0 1.9 %collective-permute-start.16 = (bf16[48,4096]{1,0:T(8,128)(2,1)S(1)}, bf16[48,4096]{1,0:T(8,128)(2,1)S(1)}, u32[]{:S(2)}, u32[]{:S(2)}) collective-permute-start(bf16[48,4096]{1,0:T(8,128)(2,1)S(1)} %get-tuple-element.21), channel_id=1, source_target_pairs={{0,64},{64,128},{128,192},{192,0},{1,65},{65,129},{129,193},{193,1... | collective-permute-start | bytes 1179656 | tf_op jit(solution)/shard_map/ppermute | solution.py:84
  92.3 2.1 %collective-permute-start.18 = (bf16[48,4096]{1,0:T(8,128)(2,1)S(1)}, bf16[48,4096]{1,0:T(8,128)(2,1)S(1)}, u32[]{:S(2)}, u32[]{:S(2)}) collective-permute-start(bf16[48,4096]{1,0:T(8,128)(2,1)S(1)} %get-tuple-element.26), channel_id=1, source_target_pairs={{0,64},{64,128},{128,192},{192,0},{1,65},{65,129},{129,193},{193,1... | collective-permute-start | bytes 1179656 | tf_op jit(solution)/shard_map/ppermute | solution.py:84
  98.6 4.1 %collective-permute-done.18 = bf16[48,4096]{1,0:T(8,128)(2,1)S(1)} collective-permute-done((bf16[48,4096]{1,0:T(8,128)(2,1)S(1)}, bf16[48,4096]{1,0:T(8,128)(2,1)S(1)}, u32[]{:S(2)}, u32[]{:S(2)}) %collective-permute-start.18) | collective-permute-done | bytes 393248 | tf_op jit(solution)/shard_map/ppermute | solution.py:84
  104.8 8.5 %all-to-all-start.1 = ((bf16[32,3,32,128]{3,2,1,0:T(8,128)(2,1)}), bf16[32,3,32,128]{3,2,1,0:T(8,128)(2,1)S(1)}, u32[]{:S(2)}, u32[]{:S(2)}) async-start(bf16[32,3,32,128]{3,2,1,0:T(8,128)(2,1)} %bitcast.56), calls=%async_computation.1 | async-start | bytes 1572864 | tf_op jit(solution)/shard_map/all_to_all | solution.py:100
  114.5 2.1 %collective-permute-start.5 = (bf16[8,4096]{1,0:T(8,128)(2,1)S(1)}, bf16[8,4096]{1,0:T(8,128)(2,1)S(1)}, u32[]{:S(2)}, u32[]{:S(2)}) collective-permute-start(bf16[8,4096]{1,0:T(8,128)(2,1)S(1)} %get-tuple-element.31), channel_id=1, source_target_pairs={{0,192},{64,0},{128,64},{192,128},{1,193},{65,1},{129,65},{193,129... | collective-permute-start | bytes 196616 | tf_op jit(solution)/shard_map/ppermute | solution.py:84
  118.8 3.6 %collective-permute-done.6 = bf16[8,4096]{1,0:T(8,128)(2,1)S(1)} collective-permute-done((bf16[8,4096]{1,0:T(8,128)(2,1)S(1)}, bf16[8,4096]{1,0:T(8,128)(2,1)S(1)}, u32[]{:S(2)}, u32[]{:S(2)}) %collective-permute-start.6) | collective-permute-done | bytes 65568 | tf_op jit(solution)/shard_map/ppermute | solution.py:84
  123.0 8.0 %all-to-all-done.1 = bf16[32,3,32,128]{3,2,1,0:T(8,128)(2,1)S(1)} async-done(((bf16[32,3,32,128]{3,2,1,0:T(8,128)(2,1)}), bf16[32,3,32,128]{3,2,1,0:T(8,128)(2,1)S(1)}, u32[]{:S(2)}, u32[]{:S(2)}) %all-to-all-start.1) | async-done | bytes 786464 | tf_op jit(solution)/shard_map/all_to_all | solution.py:100
  (76 shorter events, 31.6 us)
Async XLA Ops:
  0.0 30.1 %copy-start = (bf16[256,4096]{1,0:T(8,128)(2,1)S(1)}, bf16[256,4096]{1,0:T(8,128)(2,1)}, u32[]{:S(2)}) copy-start(bf16[256,4096]{1,0:T(8,128)(2,1)} %param.17) | copy-start | bytes 6291460
  3.7 19.0 %collective-permute-start = (bf16[8,4096]{1,0:T(8,128)(2,1)}, bf16[8,4096]{1,0:T(8,128)(2,1)S(1)}, u32[]{:S(2)}, u32[]{:S(2)}) collective-permute-start(bf16[8,4096]{1,0:T(8,128)(2,1)} %param.9), channel_id=1, source_target_pairs={{0,64},{64,128},{128,192},{192,0},{1,65},{65,129},{129,193},{193,1... | collective-permute-start | bytes 196616 | tf_op jit(solution)/shard_map/ppermute | solution.py:84
  5.4 17.4 %collective-permute-start.1 = (bf16[8,4096]{1,0:T(8,128)(2,1)}, bf16[8,4096]{1,0:T(8,128)(2,1)S(1)}, u32[]{:S(2)}, u32[]{:S(2)}) collective-permute-start(bf16[8,4096]{1,0:T(8,128)(2,1)} %param.9), channel_id=1, source_target_pairs={{0,128},{64,192},{128,0},{192,64},{1,129},{65,193},{129,1},{193,65... | collective-permute-start | bytes 196616 | tf_op jit(solution)/shard_map/ppermute | solution.py:84
  8.3 14.5 %collective-permute-start.2 = (bf16[8,4096]{1,0:T(8,128)(2,1)}, bf16[8,4096]{1,0:T(8,128)(2,1)S(1)}, u32[]{:S(2)}, u32[]{:S(2)}) collective-permute-start(bf16[8,4096]{1,0:T(8,128)(2,1)} %param.9), channel_id=1, source_target_pairs={{0,192},{64,0},{128,64},{192,128},{1,193},{65,1},{129,65},{193,129... | collective-permute-start | bytes 196616 | tf_op jit(solution)/shard_map/ppermute | solution.py:84
  9.6 35.8 %collective-permute-start.8 = (bf16[4096,256]{1,0:T(8,128)(2,1)}, bf16[4096,256]{1,0:T(8,128)(2,1)}, u32[]{:S(2)}, u32[]{:S(2)}) collective-permute-start(bf16[4096,256]{1,0:T(8,128)(2,1)} %bitcast.57), channel_id=1, source_target_pairs={{0,32},{32,0},{1,33},{33,1},{2,34},{34,2},{3,35},{35,3},{4,36},{36... | collective-permute-start | bytes 6291464 | tf_op jit(solution)/shard_map/ppermute | solution.py:84
  9.6 40.9 %collective-permute-start.9 = (bf16[4096,256]{1,0:T(8,128)(2,1)}, bf16[4096,256]{1,0:T(8,128)(2,1)}, u32[]{:S(2)}, u32[]{:S(2)}) collective-permute-start(bf16[4096,256]{1,0:T(8,128)(2,1)} %bitcast.59), channel_id=1, source_target_pairs={{0,32},{32,0},{1,33},{33,1},{2,34},{34,2},{3,35},{35,3},{4,36},{36... | collective-permute-start | bytes 6291464 | tf_op jit(solution)/shard_map/ppermute | solution.py:84
  10.2 34.2 %all-to-all-start = ((bf16[32,3,32,128]{3,2,1,0:T(8,128)(2,1)}), bf16[32,3,32,128]{3,2,1,0:T(8,128)(2,1)S(1)}, u32[]{:S(2)}, u32[]{:S(2)}) async-start(bf16[32,3,32,128]{3,2,1,0:T(8,128)(2,1)} %bitcast), calls=%async_computation | async-start | bytes 1572864 | tf_op jit(solution)/shard_map/all_to_all | solution.py:100
  22.8 29.9 %collective-permute-start.10 = (bf16[256,4096]{1,0:T(8,128)(2,1)}, bf16[256,4096]{1,0:T(8,128)(2,1)}, u32[]{:S(2)}, u32[]{:S(2)}) collective-permute-start(bf16[256,4096]{1,0:T(8,128)(2,1)} %bitcast.61), channel_id=1, source_target_pairs={{0,32},{32,0},{1,33},{33,1},{2,34},{34,2},{3,35},{35,3},{4,36},{36... | collective-permute-start | bytes 6291464 | tf_op jit(solution)/shard_map/ppermute | solution.py:84
  23.7 3.8 %collective-permute-start.3 = (bf16[32,4096]{1,0:T(8,128)(2,1)S(1)}, bf16[32,4096]{1,0:T(8,128)(2,1)S(1)}, u32[]{:S(2)}, u32[]{:S(2)}) collective-permute-start(bf16[32,4096]{1,0:T(8,128)(2,1)S(1)} %pad_maximum_fusion.8), channel_id=1, source_target_pairs={{0,32},{32,0},{1,33},{33,1},{2,34},{34,2},{3,35},{35,3},{4,36},{36... | collective-permute-start | bytes 786440 | tf_op jit(solution)/shard_map/ppermute | solution.py:84
  32.6 80.7 %collective-permute-start.4 = (bf16[32,4096]{1,0:T(8,128)(2,1)S(1)}, bf16[32,4096]{1,0:T(8,128)(2,1)S(1)}, u32[]{:S(2)}, u32[]{:S(2)}) collective-permute-start(bf16[32,4096]{1,0:T(8,128)(2,1)S(1)} %slice.119), channel_id=1, source_target_pairs={{0,32},{32,0},{1,33},{33,1},{2,34},{34,2},{3,35},{35,3},{4,36},{36... | collective-permute-start | bytes 786440 | tf_op jit(solution)/shard_map/ppermute | solution.py:84
  44.7 19.0 %collective-permute-start.11 = (bf16[96,4096]{1,0:T(8,128)(2,1)S(1)}, bf16[96,4096]{1,0:T(8,128)(2,1)S(1)}, u32[]{:S(2)}, u32[]{:S(2)}) collective-permute-start(bf16[96,4096]{1,0:T(8,128)(2,1)S(1)} %bitcast.63), channel_id=1, source_target_pairs={{0,64},{64,128},{128,192},{192,0},{1,65},{65,129},{129,193},{193,1... | collective-permute-start | bytes 2359304 | tf_op jit(solution)/shard_map/ppermute | solution.py:84
  45.5 18.4 %collective-permute-start.12 = (bf16[96,4096]{1,0:T(8,128)(2,1)S(1)}, bf16[96,4096]{1,0:T(8,128)(2,1)S(1)}, u32[]{:S(2)}, u32[]{:S(2)}) collective-permute-start(bf16[96,4096]{1,0:T(8,128)(2,1)S(1)} %bitcast.64), channel_id=1, source_target_pairs={{0,192},{64,0},{128,64},{192,128},{1,193},{65,1},{129,65},{193,129... | collective-permute-start | bytes 2359304 | tf_op jit(solution)/shard_map/ppermute | solution.py:84
  63.8 9.7 %collective-permute-start.13 = (bf16[48,4096]{1,0:T(8,128)(2,1)S(1)}, bf16[48,4096]{1,0:T(8,128)(2,1)S(1)}, u32[]{:S(2)}, u32[]{:S(2)}) collective-permute-start(bf16[48,4096]{1,0:T(8,128)(2,1)S(1)} %get-tuple-element.27), channel_id=1, source_target_pairs={{0,64},{64,128},{128,192},{192,0},{1,65},{65,129},{129,193},{193,1... | collective-permute-start | bytes 1179656 | tf_op jit(solution)/shard_map/ppermute | solution.py:84
  63.9 9.6 %collective-permute-start.14 = (bf16[48,4096]{1,0:T(8,128)(2,1)S(1)}, bf16[48,4096]{1,0:T(8,128)(2,1)S(1)}, u32[]{:S(2)}, u32[]{:S(2)}) collective-permute-start(bf16[48,4096]{1,0:T(8,128)(2,1)S(1)} %get-tuple-element.29), channel_id=1, source_target_pairs={{0,192},{64,0},{128,64},{192,128},{1,193},{65,1},{129,65},{193,129... | collective-permute-start | bytes 1179656 | tf_op jit(solution)/shard_map/ppermute | solution.py:84
  76.0 9.6 %collective-permute-start.15 = (bf16[48,4096]{1,0:T(8,128)(2,1)S(1)}, bf16[48,4096]{1,0:T(8,128)(2,1)S(1)}, u32[]{:S(2)}, u32[]{:S(2)}) collective-permute-start(bf16[48,4096]{1,0:T(8,128)(2,1)S(1)} %get-tuple-element.23), channel_id=1, source_target_pairs={{0,64},{64,128},{128,192},{192,0},{1,65},{65,129},{129,193},{193,1... | collective-permute-start | bytes 1179656 | tf_op jit(solution)/shard_map/ppermute | solution.py:84
  76.1 12.8 %collective-permute-start.19 = (bf16[48,4096]{1,0:T(8,128)(2,1)S(1)}, bf16[48,4096]{1,0:T(8,128)(2,1)S(1)}, u32[]{:S(2)}, u32[]{:S(2)}) collective-permute-start(bf16[48,4096]{1,0:T(8,128)(2,1)S(1)} %get-tuple-element.24), channel_id=1, source_target_pairs={{0,192},{64,0},{128,64},{192,128},{1,193},{65,1},{129,65},{193,129... | collective-permute-start | bytes 1179656 | tf_op jit(solution)/shard_map/ppermute | solution.py:84
  79.4 17.4 %collective-permute-start.17 = (bf16[48,4096]{1,0:T(8,128)(2,1)S(1)}, bf16[48,4096]{1,0:T(8,128)(2,1)S(1)}, u32[]{:S(2)}, u32[]{:S(2)}) collective-permute-start(bf16[48,4096]{1,0:T(8,128)(2,1)S(1)} %get-tuple-element.25), channel_id=1, source_target_pairs={{0,192},{64,0},{128,64},{192,128},{1,193},{65,1},{129,65},{193,129... | collective-permute-start | bytes 1179656 | tf_op jit(solution)/shard_map/ppermute | solution.py:84
  89.0 9.5 %collective-permute-start.16 = (bf16[48,4096]{1,0:T(8,128)(2,1)S(1)}, bf16[48,4096]{1,0:T(8,128)(2,1)S(1)}, u32[]{:S(2)}, u32[]{:S(2)}) collective-permute-start(bf16[48,4096]{1,0:T(8,128)(2,1)S(1)} %get-tuple-element.21), channel_id=1, source_target_pairs={{0,64},{64,128},{128,192},{192,0},{1,65},{65,129},{129,193},{193,1... | collective-permute-start | bytes 1179656 | tf_op jit(solution)/shard_map/ppermute | solution.py:84
  92.3 10.5 %collective-permute-start.18 = (bf16[48,4096]{1,0:T(8,128)(2,1)S(1)}, bf16[48,4096]{1,0:T(8,128)(2,1)S(1)}, u32[]{:S(2)}, u32[]{:S(2)}) collective-permute-start(bf16[48,4096]{1,0:T(8,128)(2,1)S(1)} %get-tuple-element.26), channel_id=1, source_target_pairs={{0,64},{64,128},{128,192},{192,0},{1,65},{65,129},{129,193},{193,1... | collective-permute-start | bytes 1179656 | tf_op jit(solution)/shard_map/ppermute | solution.py:84
  94.4 8.4 %collective-permute-start.20 = (bf16[48,4096]{1,0:T(8,128)(2,1)S(1)}, bf16[48,4096]{1,0:T(8,128)(2,1)S(1)}, u32[]{:S(2)}, u32[]{:S(2)}) collective-permute-start(bf16[48,4096]{1,0:T(8,128)(2,1)S(1)} %get-tuple-element.22), channel_id=1, source_target_pairs={{0,192},{64,0},{128,64},{192,128},{1,193},{65,1},{129,65},{193,129... | collective-permute-start | bytes 1179656 | tf_op jit(solution)/shard_map/ppermute | solution.py:84
  104.8 26.2 %all-to-all-start.1 = ((bf16[32,3,32,128]{3,2,1,0:T(8,128)(2,1)}), bf16[32,3,32,128]{3,2,1,0:T(8,128)(2,1)S(1)}, u32[]{:S(2)}, u32[]{:S(2)}) async-start(bf16[32,3,32,128]{3,2,1,0:T(8,128)(2,1)} %bitcast.56), calls=%async_computation.1 | async-start | bytes 1572864 | tf_op jit(solution)/shard_map/all_to_all | solution.py:100
  114.5 4.3 %collective-permute-start.5 = (bf16[8,4096]{1,0:T(8,128)(2,1)S(1)}, bf16[8,4096]{1,0:T(8,128)(2,1)S(1)}, u32[]{:S(2)}, u32[]{:S(2)}) collective-permute-start(bf16[8,4096]{1,0:T(8,128)(2,1)S(1)} %get-tuple-element.31), channel_id=1, source_target_pairs={{0,192},{64,0},{128,64},{192,128},{1,193},{65,1},{129,65},{193,129... | collective-permute-start | bytes 196616 | tf_op jit(solution)/shard_map/ppermute | solution.py:84
  116.5 5.9 %collective-permute-start.6 = (bf16[8,4096]{1,0:T(8,128)(2,1)S(1)}, bf16[8,4096]{1,0:T(8,128)(2,1)S(1)}, u32[]{:S(2)}, u32[]{:S(2)}) collective-permute-start(bf16[8,4096]{1,0:T(8,128)(2,1)S(1)} %get-tuple-element.33), channel_id=1, source_target_pairs={{0,128},{64,192},{128,0},{192,64},{1,129},{65,193},{129,1},{193,65... | collective-permute-start | bytes 196616 | tf_op jit(solution)/shard_map/ppermute | solution.py:84
  116.7 6.2 %collective-permute-start.7 = (bf16[8,4096]{1,0:T(8,128)(2,1)S(1)}, bf16[8,4096]{1,0:T(8,128)(2,1)S(1)}, u32[]{:S(2)}, u32[]{:S(2)}) collective-permute-start(bf16[8,4096]{1,0:T(8,128)(2,1)S(1)} %get-tuple-element.32), channel_id=1, source_target_pairs={{0,64},{64,128},{128,192},{192,0},{1,65},{65,129},{129,193},{193,1... | collective-permute-start | bytes 196616 | tf_op jit(solution)/shard_map/ppermute | solution.py:84
  (5 other events, 43.9 us)

commit v3 on v2

--- a/solution.py
+++ b/solution.py
@@ -18,15 +18,26 @@
     return pl.BlockSpec(memory_space=pltpu.VMEM)
 
 
-def pack_rows(ids, rows3, experts, order):
+def pack_rows(ids, rows, experts, order):
     count, picks = ids.shape
+    folds = rows.shape[1] // LANES
 
-    def kernel(ids_ref, rows_ref, out_ref, slot_ref, used_ref):
+    def kernel(ids_hbm, rows_hbm, out_ref, slot_ref, ids_ref, rows_ref, rows3_ref, used_ref, sems):
+        copies = (
+            pltpu.make_async_copy(ids_hbm, ids_ref, sems.at[0]),
+            pltpu.make_async_copy(rows_hbm, rows_ref, sems.at[1]),
+        )
+        for copy in copies:
+            copy.start()
         out_ref[...] = jnp.zeros_like(out_ref)
         for e in range(experts):
             used_ref[e] = 0
+        for copy in copies:
+            copy.wait()
+        for c in range(folds):
+            rows3_ref[:, c, :] = rows_ref[:, c * LANES : (c + 1) * LANES].astype(jnp.float32)
         for r in range(count):
-            row = rows_ref[r]
+            row = rows3_ref[r].astype(out_ref.dtype)
             for k in range(picks):
                 e = ids_ref[r, k]
                 n = used_ref[e]
@@ -38,35 +49,47 @@
     return pl.pallas_call(
         kernel,
         out_shape=(
-            jax.ShapeDtypeStruct((experts * CAP,) + rows3.shape[1:], rows3.dtype),
+            jax.ShapeDtypeStruct((experts * CAP, folds, LANES), rows.dtype),
             jax.ShapeDtypeStruct(ids.shape, jnp.int32),
         ),
-        in_specs=[in_smem(), in_vmem()],
+        in_specs=[pl.BlockSpec(memory_space=pltpu.HBM)] * 2,
         out_specs=(in_vmem(), in_smem()),
-        scratch_shapes=[pltpu.SMEM((experts,), jnp.int32)],
-        compiler_params=SMALL,
+        scratch_shapes=[
+            pltpu.SMEM(ids.shape, jnp.int32),
+            pltpu.VMEM(rows.shape, rows.dtype),
+            pltpu.VMEM((count, folds, LANES), jnp.float32),
+            pltpu.SMEM((experts,), jnp.int32),
+            pltpu.SemaphoreType.DMA((2,)),
+        ],
+        compiler_params=pltpu.CompilerParams(vmem_limit_bytes=62 * 2**20),
         name="pack_rows",
-    )(ids, rows3)
+    )(ids, rows)
 
 
-def combine_rows(slots, gates, shared3, returned):
+def combine_rows(slots, gates, shared, returned):
     count, picks = slots.shape
 
-    def kernel(slot_ref, gates_ref, shared_ref, ret_ref, out_ref):
+    folds = returned.shape[1]
+
+    def kernel(slot_ref, gates_ref, shared_ref, ret_ref, out_ref, routed_ref):
         for r in range(count):
-            total = shared_ref[r]
-            for k in range(picks):
+            total = gates_ref[r, 0] * ret_ref[slot_ref[r, 0]].astype(jnp.float32)
+            for k in range(1, picks):
                 total = total + gates_ref[r, k] * ret_ref[slot_ref[r, k]].astype(jnp.float32)
-            out_ref[r] = total.astype(out_ref.dtype)
+            routed_ref[r] = total
+        for c in range(folds):
+            part = slice(c * LANES, (c + 1) * LANES)
+            out_ref[:, part] = (shared_ref[:, part] + routed_ref[:, c, :]).astype(out_ref.dtype)
 
     return pl.pallas_call(
         kernel,
-        out_shape=jax.ShapeDtypeStruct(shared3.shape, jnp.bfloat16),
+        out_shape=jax.ShapeDtypeStruct(shared.shape, jnp.bfloat16),
         in_specs=[in_smem(), in_smem(), in_vmem(), in_vmem()],
         out_specs=in_vmem(),
+        scratch_shapes=[pltpu.VMEM((count, folds, LANES), jnp.float32)],
         compiler_params=SMALL,
         name="combine_rows",
-    )(slots, gates, shared3, returned)
+    )(slots, gates, shared, returned)
 
 
 def hidden_of(rows, gate_w, up_w):
@@ -100,7 +123,7 @@
         arrived = lax.all_to_all(rows.reshape(split), ("z", "x"), split_axis=0, concat_axis=0, tiled=True)
         return arrived.reshape(slots, part, LANES)
 
-    packed, places = pack_rows(ids, tokens.reshape(own, folds, LANES), experts, by_z)
+    packed, places = pack_rows(ids, tokens, experts, by_z)
     early, packed = lax.optimization_barrier((tokens, packed))
 
     own_w = (w_gate[0], w_up[0], w_down[0])
@@ -143,8 +166,7 @@
     total = total + jnp.concatenate(back, axis=0)
     returned = exchange(total.astype(jnp.bfloat16), folds)
 
-    mixed = combine_rows(places, gates, shared.reshape(own, folds, LANES), returned)
-    return mixed.reshape(own, width)
+    return combine_rows(places, gates, shared, returned)
 
 
 def solution(mesh):

time: 134 us -> 132 us (0.985)
  waiting for transfers between devices: 53.6 us -> 57 us
  local copies, waits for them, and re-layouts: 6.26 us -> 3.71 us
  matrix products: 12.1 us -> 9.64 us
    all_to_all x2, waiting for transfers between devices: 19.5 us -> 24.3 us  [exchange(): lax.all_to_all(rows.reshape(split), ('z', 'x'), split_axis=0, concat_axis...]
    dot_general x4, matrix products: 4.5 us -> 2.92 us  [hidden_of(): gate = jnp.dot(rows, gate_w, preferred_element_type=jnp.float32)]
    unnamed x22 -> x23, local copies, waits for them, and re-layouts: 4.92 us -> 3.41 us
    ppermute x21, waiting for transfers between devices: 34.1 us -> 32.7 us  [shift(): return lax.ppermute(value, axis, [(i, (i + by) % n) for i in range(n)])]
  transfers between devices with their start and end apart: 23 -> 23, of which waited for: 13 -> 14; matrix products, arithmetic and copies ran while one was open for 19% -> 13% of each run, Pallas kernels for 0% -> 0%
where the time goes in v3:
time: 132 us; the launch traced here: 131 us
  waiting for transfers between devices  57 us (43%)
  starting transfers between devices  48.1 us (36%)
  matrix products  9.64 us (7%)
  other arithmetic  8.49 us (6%)
  local copies, waits for them, and re-layouts  3.71 us (3%)
  Pallas kernels  3.61 us (3%)
    ppermute x21, waiting for transfers between devices, shift(): return lax.ppermute(value, axis, [(i, (i + by) % n) for i in range(n)])  32.7 us
    ppermute x21, starting transfers between devices, shift(): return lax.ppermute(value, axis, [(i, (i + by) % n) for i in range(n)])  27.9 us
    all_to_all x2, waiting for transfers between devices, exchange(): lax.all_to_all(rows.reshape(split), ('z', 'x'), split_axis=0, concat_axis...  24.3 us
    all_to_all x2, starting transfers between devices, exchange(): lax.all_to_all(rows.reshape(split), ('z', 'x'), split_axis=0, concat_axis...  20.2 us
    concatenate x2, other arithmetic, layer(): jnp.concatenate(pair, axis=1)  3.79 us
    dot_general x5, matrix products, down(): return jnp.dot(hidden, down_w, preferred_element_type=jnp.float32)  3.75 us
    unnamed x23, local copies, waits for them, and re-layouts  3.41 us
    dot_general x4, matrix products, hidden_of(): up = jnp.dot(rows, up_w, preferred_element_type=jnp.float32)  2.97 us
  transfers between devices with their start and end apart: 23, of which 14 were waited for; matrix products, arithmetic and copies ran while one was open for 13% of the time, Pallas kernels for 0%

profile of v3, /device:TPU:2, one launch (start us, length us, event | category | flops | bytes accessed | tf_op | source)
XLA Modules:
  0.0 130.9 jit_solution(12601599555065763891)
XLA Ops:
  0.0 2.1 %pack_rows.1 = (bf16[96,32,128]{2,1,0:T(8,128)(2,1)}, s32[8,8]{1,0:T(8,128)}) custom-call(s32[8,8]{1,0:T(8,128)} %ids_hbm.1, bf16[8,4096]{1,0:T(8,128)(2,1)} %rows_hbm.1), custom_call_target="tpu_custom_call" | custom-call | tf_op jit(solution)/shard_map/pack_rows/pallas_call | solution.py:49
  2.1 1.7 %collective-permute-start = (bf16[8,4096]{1,0:T(8,128)(2,1)}, bf16[8,4096]{1,0:T(8,128)(2,1)S(1)}, u32[]{:S(2)}, u32[]{:S(2)}) collective-permute-start(bf16[8,4096]{1,0:T(8,128)(2,1)} %rows_hbm.1), channel_id=1, source_target_pairs={{0,64},{64,128},{128,192},{192,0},{1,65},{65,129},{129,193},{193,1... | collective-permute-start | bytes 196616 | tf_op jit(solution)/shard_map/ppermute | solution.py:107
  3.8 2.9 %collective-permute-start.1 = (bf16[8,4096]{1,0:T(8,128)(2,1)}, bf16[8,4096]{1,0:T(8,128)(2,1)S(1)}, u32[]{:S(2)}, u32[]{:S(2)}) collective-permute-start(bf16[8,4096]{1,0:T(8,128)(2,1)} %rows_hbm.1), channel_id=1, source_target_pairs={{0,128},{64,192},{128,0},{192,64},{1,129},{65,193},{129,1},{193,65... | collective-permute-start | bytes 196616 | tf_op jit(solution)/shard_map/ppermute | solution.py:107
  8.6 11.6 %all-to-all-start = ((bf16[32,3,32,128]{3,2,1,0:T(8,128)(2,1)}), bf16[32,3,32,128]{3,2,1,0:T(8,128)(2,1)S(1)}, u32[]{:S(2)}, u32[]{:S(2)}) async-start(bf16[32,3,32,128]{3,2,1,0:T(8,128)(2,1)} %bitcast.44), calls=%async_computation | async-start | bytes 1572864 | tf_op jit(solution)/shard_map/all_to_all | solution.py:123
  27.6 15.2 %all-to-all-done = bf16[32,3,32,128]{3,2,1,0:T(8,128)(2,1)S(1)} async-done(((bf16[32,3,32,128]{3,2,1,0:T(8,128)(2,1)}), bf16[32,3,32,128]{3,2,1,0:T(8,128)(2,1)S(1)}, u32[]{:S(2)}, u32[]{:S(2)}) %all-to-all-start) | async-done | bytes 786464 | tf_op jit(solution)/shard_map/all_to_all | solution.py:123
  43.9 2.6 %collective-permute-start.12 = (bf16[96,4096]{1,0:T(8,128)(2,1)S(1)}, bf16[96,4096]{1,0:T(8,128)(2,1)S(1)}, u32[]{:S(2)}, u32[]{:S(2)}) collective-permute-start(bf16[96,4096]{1,0:T(8,128)(2,1)S(1)} %bitcast.46), channel_id=1, source_target_pairs={{0,192},{64,0},{128,64},{192,128},{1,193},{65,1},{129,65},{193,129... | collective-permute-start | bytes 2359304 | tf_op jit(solution)/shard_map/ppermute | solution.py:107
  46.5 1.9 %pad_maximum_fusion = bf16[4096,512]{1,0:T(8,128)(2,1)S(1)} fusion(bf16[4096,256]{1,0:T(8,128)(2,1)} %collective-permute-done.8, bf16[4096,256]{1,0:T(8,128)(2,1)S(1)} %bitcast.41), kind=kLoop, calls=%fused_computation.2 | loop fusion | flops 8388608 | bytes 8388608 | tf_op jit(solution)/shard_map/concatenate | solution.py:131
  48.4 1.9 %pad_maximum_fusion.1 = bf16[4096,512]{1,0:T(8,128)(2,1)S(1)} fusion(bf16[4096,256]{1,0:T(8,128)(2,1)} %collective-permute-done.9, bf16[4096,256]{1,0:T(8,128)(2,1)S(1)} %bitcast.43), kind=kLoop, calls=%fused_computation.3 | loop fusion | flops 8388608 | bytes 8388608 | tf_op jit(solution)/shard_map/concatenate | solution.py:131
  50.3 2.7 %pad_maximum_fusion.2 = bf16[512,4096]{1,0:T(8,128)(2,1)S(1)} fusion(bf16[256,4096]{1,0:T(8,128)(2,1)} %collective-permute-done.10, bf16[256,4096]{1,0:T(8,128)(2,1)} %bitcast.3), kind=kLoop, calls=%fused_computation.4 | loop fusion | flops 8388608 | bytes 8388608 | tf_op jit(solution)/shard_map/concatenate | solution.py:132
  53.0 9.1 %collective-permute-done.11 = bf16[96,4096]{1,0:T(8,128)(2,1)S(1)} collective-permute-done((bf16[96,4096]{1,0:T(8,128)(2,1)S(1)}, bf16[96,4096]{1,0:T(8,128)(2,1)S(1)}, u32[]{:S(2)}, u32[]{:S(2)}) %collective-permute-start.11) | collective-permute-done | bytes 786464 | tf_op jit(solution)/shard_map/ppermute | solution.py:107
  62.3 3.5 %collective-permute-start.14 = (bf16[48,4096]{1,0:T(8,128)(2,1)S(1)}, bf16[48,4096]{1,0:T(8,128)(2,1)S(1)}, u32[]{:S(2)}, u32[]{:S(2)}) collective-permute-start(bf16[48,4096]{1,0:T(8,128)(2,1)S(1)} %get-tuple-element.29), channel_id=1, source_target_pairs={{0,192},{64,0},{128,64},{192,128},{1,193},{65,1},{129,65},{193,129... | collective-permute-start | bytes 1179656 | tf_op jit(solution)/shard_map/ppermute | solution.py:107
  68.6 3.3 %collective-permute-done.13 = bf16[48,4096]{1,0:T(8,128)(2,1)S(1)} collective-permute-done((bf16[48,4096]{1,0:T(8,128)(2,1)S(1)}, bf16[48,4096]{1,0:T(8,128)(2,1)S(1)}, u32[]{:S(2)}, u32[]{:S(2)}) %collective-permute-start.13) | collective-permute-done | bytes 393248 | tf_op jit(solution)/shard_map/ppermute | solution.py:107
  74.5 3.3 %collective-permute-start.19 = (bf16[48,4096]{1,0:T(8,128)(2,1)S(1)}, bf16[48,4096]{1,0:T(8,128)(2,1)S(1)}, u32[]{:S(2)}, u32[]{:S(2)}) collective-permute-start(bf16[48,4096]{1,0:T(8,128)(2,1)S(1)} %get-tuple-element.24), channel_id=1, source_target_pairs={{0,192},{64,0},{128,64},{192,128},{1,193},{65,1},{129,65},{193,129... | collective-permute-start | bytes 1179656 | tf_op jit(solution)/shard_map/ppermute | solution.py:107
  77.9 2.0 %collective-permute-start.17 = (bf16[48,4096]{1,0:T(8,128)(2,1)S(1)}, bf16[48,4096]{1,0:T(8,128)(2,1)S(1)}, u32[]{:S(2)}, u32[]{:S(2)}) collective-permute-start(bf16[48,4096]{1,0:T(8,128)(2,1)S(1)} %get-tuple-element.25), channel_id=1, source_target_pairs={{0,192},{64,0},{128,64},{192,128},{1,193},{65,1},{129,65},{193,129... | collective-permute-start | bytes 1179656 | tf_op jit(solution)/shard_map/ppermute | solution.py:107
  80.7 3.3 %collective-permute-done.15 = bf16[48,4096]{1,0:T(8,128)(2,1)S(1)} collective-permute-done((bf16[48,4096]{1,0:T(8,128)(2,1)S(1)}, bf16[48,4096]{1,0:T(8,128)(2,1)S(1)}, u32[]{:S(2)}, u32[]{:S(2)}) %collective-permute-start.15) | collective-permute-done | bytes 393248 | tf_op jit(solution)/shard_map/ppermute | solution.py:107
  84.0 3.3 %collective-permute-done.19 = bf16[48,4096]{1,0:T(8,128)(2,1)S(1)} collective-permute-done((bf16[48,4096]{1,0:T(8,128)(2,1)S(1)}, bf16[48,4096]{1,0:T(8,128)(2,1)S(1)}, u32[]{:S(2)}, u32[]{:S(2)}) %collective-permute-start.19) | collective-permute-done | bytes 393248 | tf_op jit(solution)/shard_map/ppermute | solution.py:107
  87.5 1.9 %collective-permute-start.16 = (bf16[48,4096]{1,0:T(8,128)(2,1)S(1)}, bf16[48,4096]{1,0:T(8,128)(2,1)S(1)}, u32[]{:S(2)}, u32[]{:S(2)}) collective-permute-start(bf16[48,4096]{1,0:T(8,128)(2,1)S(1)} %get-tuple-element.21), channel_id=1, source_target_pairs={{0,64},{64,128},{128,192},{192,0},{1,65},{65,129},{129,193},{193,1... | collective-permute-start | bytes 1179656 | tf_op jit(solution)/shard_map/ppermute | solution.py:107
  90.8 2.1 %collective-permute-start.18 = (bf16[48,4096]{1,0:T(8,128)(2,1)S(1)}, bf16[48,4096]{1,0:T(8,128)(2,1)S(1)}, u32[]{:S(2)}, u32[]{:S(2)}) collective-permute-start(bf16[48,4096]{1,0:T(8,128)(2,1)S(1)} %get-tuple-element.26), channel_id=1, source_target_pairs={{0,64},{64,128},{128,192},{192,0},{1,65},{65,129},{129,193},{193,1... | collective-permute-start | bytes 1179656 | tf_op jit(solution)/shard_map/ppermute | solution.py:107
  95.2 1.8 %collective-permute-done.16 = bf16[48,4096]{1,0:T(8,128)(2,1)S(1)} collective-permute-done((bf16[48,4096]{1,0:T(8,128)(2,1)S(1)}, bf16[48,4096]{1,0:T(8,128)(2,1)S(1)}, u32[]{:S(2)}, u32[]{:S(2)}) %collective-permute-start.16) | collective-permute-done | bytes 393248 | tf_op jit(solution)/shard_map/ppermute | solution.py:107
  97.1 4.1 %collective-permute-done.18 = bf16[48,4096]{1,0:T(8,128)(2,1)S(1)} collective-permute-done((bf16[48,4096]{1,0:T(8,128)(2,1)S(1)}, bf16[48,4096]{1,0:T(8,128)(2,1)S(1)}, u32[]{:S(2)}, u32[]{:S(2)}) %collective-permute-start.18) | collective-permute-done | bytes 393248 | tf_op jit(solution)/shard_map/ppermute | solution.py:107
  103.2 8.5 %all-to-all-start.1 = ((bf16[32,3,32,128]{3,2,1,0:T(8,128)(2,1)}), bf16[32,3,32,128]{3,2,1,0:T(8,128)(2,1)S(1)}, u32[]{:S(2)}, u32[]{:S(2)}) async-start(bf16[32,3,32,128]{3,2,1,0:T(8,128)(2,1)} %bitcast.10), calls=%async_computation.1 | async-start | bytes 1572864 | tf_op jit(solution)/shard_map/all_to_all | solution.py:123
  111.8 2.1 %collective-permute-start.5 = (bf16[8,4096]{1,0:T(8,128)(2,1)S(1)}, bf16[8,4096]{1,0:T(8,128)(2,1)S(1)}, u32[]{:S(2)}, u32[]{:S(2)}) collective-permute-start(bf16[8,4096]{1,0:T(8,128)(2,1)S(1)} %get-tuple-element.31), channel_id=1, source_target_pairs={{0,192},{64,0},{128,64},{192,128},{1,193},{65,1},{129,65},{193,129... | collective-permute-start | bytes 196616 | tf_op jit(solution)/shard_map/ppermute | solution.py:107
  116.2 3.6 %collective-permute-done.6 = bf16[8,4096]{1,0:T(8,128)(2,1)S(1)} collective-permute-done((bf16[8,4096]{1,0:T(8,128)(2,1)S(1)}, bf16[8,4096]{1,0:T(8,128)(2,1)S(1)}, u32[]{:S(2)}, u32[]{:S(2)}) %collective-permute-start.6) | collective-permute-done | bytes 65568 | tf_op jit(solution)/shard_map/ppermute | solution.py:107
  120.3 9.1 %all-to-all-done.1 = bf16[32,3,32,128]{3,2,1,0:T(8,128)(2,1)S(1)} async-done(((bf16[32,3,32,128]{3,2,1,0:T(8,128)(2,1)}), bf16[32,3,32,128]{3,2,1,0:T(8,128)(2,1)S(1)}, u32[]{:S(2)}, u32[]{:S(2)}) %all-to-all-start.1) | async-done | bytes 786464 | tf_op jit(solution)/shard_map/all_to_all | solution.py:123
  (77 shorter events, 27.0 us)
Async XLA Ops:
  2.1 19.0 %collective-permute-start = (bf16[8,4096]{1,0:T(8,128)(2,1)}, bf16[8,4096]{1,0:T(8,128)(2,1)S(1)}, u32[]{:S(2)}, u32[]{:S(2)}) collective-permute-start(bf16[8,4096]{1,0:T(8,128)(2,1)} %rows_hbm.1), channel_id=1, source_target_pairs={{0,64},{64,128},{128,192},{192,0},{1,65},{65,129},{129,193},{193,1... | collective-permute-start | bytes 196616 | tf_op jit(solution)/shard_map/ppermute | solution.py:107
  3.8 17.4 %collective-permute-start.1 = (bf16[8,4096]{1,0:T(8,128)(2,1)}, bf16[8,4096]{1,0:T(8,128)(2,1)S(1)}, u32[]{:S(2)}, u32[]{:S(2)}) collective-permute-start(bf16[8,4096]{1,0:T(8,128)(2,1)} %rows_hbm.1), channel_id=1, source_target_pairs={{0,128},{64,192},{128,0},{192,64},{1,129},{65,193},{129,1},{193,65... | collective-permute-start | bytes 196616 | tf_op jit(solution)/shard_map/ppermute | solution.py:107
  6.7 14.5 %collective-permute-start.2 = (bf16[8,4096]{1,0:T(8,128)(2,1)}, bf16[8,4096]{1,0:T(8,128)(2,1)}, u32[]{:S(2)}, u32[]{:S(2)}) collective-permute-start(bf16[8,4096]{1,0:T(8,128)(2,1)} %rows_hbm.1), channel_id=1, source_target_pairs={{0,192},{64,0},{128,64},{192,128},{1,193},{65,1},{129,65},{193,129... | collective-permute-start | bytes 196616 | tf_op jit(solution)/shard_map/ppermute | solution.py:107
  8.1 38.4 %collective-permute-start.8 = (bf16[4096,256]{1,0:T(8,128)(2,1)}, bf16[4096,256]{1,0:T(8,128)(2,1)}, u32[]{:S(2)}, u32[]{:S(2)}) collective-permute-start(bf16[4096,256]{1,0:T(8,128)(2,1)} %bitcast.40), channel_id=1, source_target_pairs={{0,32},{32,0},{1,33},{33,1},{2,34},{34,2},{3,35},{35,3},{4,36},{36... | collective-permute-start | bytes 6291464 | tf_op jit(solution)/shard_map/ppermute | solution.py:107
  8.1 40.3 %collective-permute-start.9 = (bf16[4096,256]{1,0:T(8,128)(2,1)}, bf16[4096,256]{1,0:T(8,128)(2,1)}, u32[]{:S(2)}, u32[]{:S(2)}) collective-permute-start(bf16[4096,256]{1,0:T(8,128)(2,1)} %bitcast.42), channel_id=1, source_target_pairs={{0,32},{32,0},{1,33},{33,1},{2,34},{34,2},{3,35},{35,3},{4,36},{36... | collective-permute-start | bytes 6291464 | tf_op jit(solution)/shard_map/ppermute | solution.py:107
  8.6 34.2 %all-to-all-start = ((bf16[32,3,32,128]{3,2,1,0:T(8,128)(2,1)}), bf16[32,3,32,128]{3,2,1,0:T(8,128)(2,1)S(1)}, u32[]{:S(2)}, u32[]{:S(2)}) async-start(bf16[32,3,32,128]{3,2,1,0:T(8,128)(2,1)} %bitcast.44), calls=%async_computation | async-start | bytes 1572864 | tf_op jit(solution)/shard_map/all_to_all | solution.py:123
  22.1 1.6 %collective-permute-start.3 = (bf16[32,4096]{1,0:T(8,128)(2,1)S(1)}, bf16[32,4096]{1,0:T(8,128)(2,1)S(1)}, u32[]{:S(2)}, u32[]{:S(2)}) collective-permute-start(bf16[32,4096]{1,0:T(8,128)(2,1)S(1)} %pad_maximum_fusion.8), channel_id=1, source_target_pairs={{0,32},{32,0},{1,33},{33,1},{2,34},{34,2},{3,35},{35,3},{4,36},{36... | collective-permute-start | bytes 786440 | tf_op jit(solution)/shard_map/ppermute | solution.py:107
  25.3 1.6 %collective-permute-start.4 = (bf16[32,4096]{1,0:T(8,128)(2,1)S(1)}, bf16[32,4096]{1,0:T(8,128)(2,1)S(1)}, u32[]{:S(2)}, u32[]{:S(2)}) collective-permute-start(bf16[32,4096]{1,0:T(8,128)(2,1)S(1)} %slice.117), channel_id=1, source_target_pairs={{0,32},{32,0},{1,33},{33,1},{2,34},{34,2},{3,35},{35,3},{4,36},{36... | collective-permute-start | bytes 786440 | tf_op jit(solution)/shard_map/ppermute | solution.py:107
  25.5 24.8 %collective-permute-start.10 = (bf16[256,4096]{1,0:T(8,128)(2,1)}, bf16[256,4096]{1,0:T(8,128)(2,1)}, u32[]{:S(2)}, u32[]{:S(2)}) collective-permute-start(bf16[256,4096]{1,0:T(8,128)(2,1)} %bitcast.3), channel_id=1, source_target_pairs={{0,32},{32,0},{1,33},{33,1},{2,34},{34,2},{3,35},{35,3},{4,36},{36... | collective-permute-start | bytes 6291464 | tf_op jit(solution)/shard_map/ppermute | solution.py:107
  43.1 19.0 %collective-permute-start.11 = (bf16[96,4096]{1,0:T(8,128)(2,1)S(1)}, bf16[96,4096]{1,0:T(8,128)(2,1)S(1)}, u32[]{:S(2)}, u32[]{:S(2)}) collective-permute-start(bf16[96,4096]{1,0:T(8,128)(2,1)S(1)} %bitcast.45), channel_id=1, source_target_pairs={{0,64},{64,128},{128,192},{192,0},{1,65},{65,129},{129,193},{193,1... | collective-permute-start | bytes 2359304 | tf_op jit(solution)/shard_map/ppermute | solution.py:107
  43.9 18.4 %collective-permute-start.12 = (bf16[96,4096]{1,0:T(8,128)(2,1)S(1)}, bf16[96,4096]{1,0:T(8,128)(2,1)S(1)}, u32[]{:S(2)}, u32[]{:S(2)}) collective-permute-start(bf16[96,4096]{1,0:T(8,128)(2,1)S(1)} %bitcast.46), channel_id=1, source_target_pairs={{0,192},{64,0},{128,64},{192,128},{1,193},{65,1},{129,65},{193,129... | collective-permute-start | bytes 2359304 | tf_op jit(solution)/shard_map/ppermute | solution.py:107
  62.2 9.7 %collective-permute-start.13 = (bf16[48,4096]{1,0:T(8,128)(2,1)S(1)}, bf16[48,4096]{1,0:T(8,128)(2,1)S(1)}, u32[]{:S(2)}, u32[]{:S(2)}) collective-permute-start(bf16[48,4096]{1,0:T(8,128)(2,1)S(1)} %get-tuple-element.27), channel_id=1, source_target_pairs={{0,64},{64,128},{128,192},{192,0},{1,65},{65,129},{129,193},{193,1... | collective-permute-start | bytes 1179656 | tf_op jit(solution)/shard_map/ppermute | solution.py:107
  62.3 9.6 %collective-permute-start.14 = (bf16[48,4096]{1,0:T(8,128)(2,1)S(1)}, bf16[48,4096]{1,0:T(8,128)(2,1)S(1)}, u32[]{:S(2)}, u32[]{:S(2)}) collective-permute-start(bf16[48,4096]{1,0:T(8,128)(2,1)S(1)} %get-tuple-element.29), channel_id=1, source_target_pairs={{0,192},{64,0},{128,64},{192,128},{1,193},{65,1},{129,65},{193,129... | collective-permute-start | bytes 1179656 | tf_op jit(solution)/shard_map/ppermute | solution.py:107
  74.4 9.6 %collective-permute-start.15 = (bf16[48,4096]{1,0:T(8,128)(2,1)S(1)}, bf16[48,4096]{1,0:T(8,128)(2,1)S(1)}, u32[]{:S(2)}, u32[]{:S(2)}) collective-permute-start(bf16[48,4096]{1,0:T(8,128)(2,1)S(1)} %get-tuple-element.23), channel_id=1, source_target_pairs={{0,64},{64,128},{128,192},{192,0},{1,65},{65,129},{129,193},{193,1... | collective-permute-start | bytes 1179656 | tf_op jit(solution)/shard_map/ppermute | solution.py:107
  74.5 12.8 %collective-permute-start.19 = (bf16[48,4096]{1,0:T(8,128)(2,1)S(1)}, bf16[48,4096]{1,0:T(8,128)(2,1)S(1)}, u32[]{:S(2)}, u32[]{:S(2)}) collective-permute-start(bf16[48,4096]{1,0:T(8,128)(2,1)S(1)} %get-tuple-element.24), channel_id=1, source_target_pairs={{0,192},{64,0},{128,64},{192,128},{1,193},{65,1},{129,65},{193,129... | collective-permute-start | bytes 1179656 | tf_op jit(solution)/shard_map/ppermute | solution.py:107
  77.9 17.4 %collective-permute-start.17 = (bf16[48,4096]{1,0:T(8,128)(2,1)S(1)}, bf16[48,4096]{1,0:T(8,128)(2,1)S(1)}, u32[]{:S(2)}, u32[]{:S(2)}) collective-permute-start(bf16[48,4096]{1,0:T(8,128)(2,1)S(1)} %get-tuple-element.25), channel_id=1, source_target_pairs={{0,192},{64,0},{128,64},{192,128},{1,193},{65,1},{129,65},{193,129... | collective-permute-start | bytes 1179656 | tf_op jit(solution)/shard_map/ppermute | solution.py:107
  87.5 9.5 %collective-permute-start.16 = (bf16[48,4096]{1,0:T(8,128)(2,1)S(1)}, bf16[48,4096]{1,0:T(8,128)(2,1)S(1)}, u32[]{:S(2)}, u32[]{:S(2)}) collective-permute-start(bf16[48,4096]{1,0:T(8,128)(2,1)S(1)} %get-tuple-element.21), channel_id=1, source_target_pairs={{0,64},{64,128},{128,192},{192,0},{1,65},{65,129},{129,193},{193,1... | collective-permute-start | bytes 1179656 | tf_op jit(solution)/shard_map/ppermute | solution.py:107
  90.8 10.5 %collective-permute-start.18 = (bf16[48,4096]{1,0:T(8,128)(2,1)S(1)}, bf16[48,4096]{1,0:T(8,128)(2,1)S(1)}, u32[]{:S(2)}, u32[]{:S(2)}) collective-permute-start(bf16[48,4096]{1,0:T(8,128)(2,1)S(1)} %get-tuple-element.26), channel_id=1, source_target_pairs={{0,64},{64,128},{128,192},{192,0},{1,65},{65,129},{129,193},{193,1... | collective-permute-start | bytes 1179656 | tf_op jit(solution)/shard_map/ppermute | solution.py:107
  92.9 8.4 %collective-permute-start.20 = (bf16[48,4096]{1,0:T(8,128)(2,1)S(1)}, bf16[48,4096]{1,0:T(8,128)(2,1)S(1)}, u32[]{:S(2)}, u32[]{:S(2)}) collective-permute-start(bf16[48,4096]{1,0:T(8,128)(2,1)S(1)} %get-tuple-element.22), channel_id=1, source_target_pairs={{0,192},{64,0},{128,64},{192,128},{1,193},{65,1},{129,65},{193,129... | collective-permute-start | bytes 1179656 | tf_op jit(solution)/shard_map/ppermute | solution.py:107
  102.2 27.3 %copy-start = (f32[8,8]{1,0:T(8,128)S(1)}, f32[8,8]{1,0:T(8,128)}, u32[]{:S(2)}) copy-start(f32[8,8]{1,0:T(8,128)} %gates_ref.1) | copy-start | bytes 772
  103.2 26.2 %all-to-all-start.1 = ((bf16[32,3,32,128]{3,2,1,0:T(8,128)(2,1)}), bf16[32,3,32,128]{3,2,1,0:T(8,128)(2,1)S(1)}, u32[]{:S(2)}, u32[]{:S(2)}) async-start(bf16[32,3,32,128]{3,2,1,0:T(8,128)(2,1)} %bitcast.10), calls=%async_computation.1 | async-start | bytes 1572864 | tf_op jit(solution)/shard_map/all_to_all | solution.py:123
  111.8 4.3 %collective-permute-start.5 = (bf16[8,4096]{1,0:T(8,128)(2,1)S(1)}, bf16[8,4096]{1,0:T(8,128)(2,1)S(1)}, u32[]{:S(2)}, u32[]{:S(2)}) collective-permute-start(bf16[8,4096]{1,0:T(8,128)(2,1)S(1)} %get-tuple-element.31), channel_id=1, source_target_pairs={{0,192},{64,0},{128,64},{192,128},{1,193},{65,1},{129,65},{193,129... | collective-permute-start | bytes 196616 | tf_op jit(solution)/shard_map/ppermute | solution.py:107
  113.9 5.9 %collective-permute-start.6 = (bf16[8,4096]{1,0:T(8,128)(2,1)S(1)}, bf16[8,4096]{1,0:T(8,128)(2,1)S(1)}, u32[]{:S(2)}, u32[]{:S(2)}) collective-permute-start(bf16[8,4096]{1,0:T(8,128)(2,1)S(1)} %get-tuple-element.33), channel_id=1, source_target_pairs={{0,128},{64,192},{128,0},{192,64},{1,129},{65,193},{129,1},{193,65... | collective-permute-start | bytes 196616 | tf_op jit(solution)/shard_map/ppermute | solution.py:107
  114.1 6.2 %collective-permute-start.7 = (bf16[8,4096]{1,0:T(8,128)(2,1)S(1)}, bf16[8,4096]{1,0:T(8,128)(2,1)S(1)}, u32[]{:S(2)}, u32[]{:S(2)}) collective-permute-start(bf16[8,4096]{1,0:T(8,128)(2,1)S(1)} %get-tuple-element.32), channel_id=1, source_target_pairs={{0,64},{64,128},{128,192},{192,0},{1,65},{65,129},{129,193},{193,1... | collective-permute-start | bytes 196616 | tf_op jit(solution)/shard_map/ppermute | solution.py:107
  (7 other events, 92.1 us)

commit v4 on v3

--- a/solution.py
+++ b/solution.py
@@ -159,8 +159,10 @@
     far = down(hidden_of(far, gate_w, up_w), down_w).astype(jnp.bfloat16)
     far = shift(far[:half], "y", 1), shift(far[half:], "y", planes - 1)
     upper = (held[half:] + far[0].astype(jnp.float32)).astype(jnp.bfloat16)
-    lower = (held[:half] + far[1].astype(jnp.float32)).astype(jnp.bfloat16)
-    held = shift(upper, "y", 1), shift(lower, "y", planes - 1)
+    sent = shift(upper, "y", 1)
+    upper, last = lax.optimization_barrier((upper, far[1]))
+    lower = (held[:half] + last.astype(jnp.float32)).astype(jnp.bfloat16)
+    held = sent, shift(lower, "y", planes - 1)
     back = (held[0], free[1]), (free[0], held[1])
     back = [sum(value.astype(jnp.float32) for value in values) for values in back]
     total = total + jnp.concatenate(back, axis=0)

time: 132 us -> 133 us (level)
  waiting for transfers between devices: 57 us -> 62 us
  starting transfers between devices: 48.1 us -> 44 us
    ppermute x21, waiting for transfers between devices: 32.7 us -> 37.9 us  [shift(): return lax.ppermute(value, axis, [(i, (i + by) % n) for i in range(n)])]
    ppermute x21, starting transfers between devices: 27.9 us -> 24.6 us  [shift(): return lax.ppermute(value, axis, [(i, (i + by) % n) for i in range(n)])]
where the time goes in v4:
time: 133 us; the launch traced here: 132 us
  waiting for transfers between devices  62 us (47%)
  starting transfers between devices  44 us (33%)
  matrix products  9.64 us (7%)
  other arithmetic  8.49 us (6%)
  local copies, waits for them, and re-layouts  3.7 us (3%)
  Pallas kernels  3.61 us (3%)
    ppermute x21, waiting for transfers between devices, shift(): return lax.ppermute(value, axis, [(i, (i + by) % n) for i in range(n)])  37.9 us
    ppermute x21, starting transfers between devices, shift(): return lax.ppermute(value, axis, [(i, (i + by) % n) for i in range(n)])  24.6 us
    all_to_all x2, waiting for transfers between devices, exchange(): lax.all_to_all(rows.reshape(split), ('z', 'x'), split_axis=0, concat_axis...  24.1 us
    all_to_all x2, starting transfers between devices, exchange(): lax.all_to_all(rows.reshape(split), ('z', 'x'), split_axis=0, concat_axis...  19.4 us
    concatenate x2, other arithmetic, layer(): jnp.concatenate(pair, axis=1)  3.79 us
    dot_general x5, matrix products, down(): return jnp.dot(hidden, down_w, preferred_element_type=jnp.float32)  3.74 us
    unnamed x23, local copies, waits for them, and re-layouts  3.4 us
    dot_general x4, matrix products, hidden_of(): up = jnp.dot(rows, up_w, preferred_element_type=jnp.float32)  2.97 us
  transfers between devices with their start and end apart: 23, of which 14 were waited for; matrix products, arithmetic and copies ran while one was open for 13% of the time, Pallas kernels for 0%

profile of v4, /device:TPU:2, one launch (start us, length us, event | category | flops | bytes accessed | tf_op | source)
XLA Modules:
  0.0 131.9 jit_solution(11170924780244216150)
XLA Ops:
  0.0 2.1 %pack_rows.1 = (bf16[96,32,128]{2,1,0:T(8,128)(2,1)}, s32[8,8]{1,0:T(8,128)}) custom-call(s32[8,8]{1,0:T(8,128)} %ids_hbm.1, bf16[8,4096]{1,0:T(8,128)(2,1)} %rows_hbm.1), custom_call_target="tpu_custom_call" | custom-call | tf_op jit(solution)/shard_map/pack_rows/pallas_call | solution.py:49
  2.1 1.7 %collective-permute-start = (bf16[8,4096]{1,0:T(8,128)(2,1)}, bf16[8,4096]{1,0:T(8,128)(2,1)S(1)}, u32[]{:S(2)}, u32[]{:S(2)}) collective-permute-start(bf16[8,4096]{1,0:T(8,128)(2,1)} %rows_hbm.1), channel_id=1, source_target_pairs={{0,64},{64,128},{128,192},{192,0},{1,65},{65,129},{129,193},{193,1... | collective-permute-start | bytes 196616 | tf_op jit(solution)/shard_map/ppermute | solution.py:107
  3.8 2.9 %collective-permute-start.1 = (bf16[8,4096]{1,0:T(8,128)(2,1)}, bf16[8,4096]{1,0:T(8,128)(2,1)S(1)}, u32[]{:S(2)}, u32[]{:S(2)}) collective-permute-start(bf16[8,4096]{1,0:T(8,128)(2,1)} %rows_hbm.1), channel_id=1, source_target_pairs={{0,128},{64,192},{128,0},{192,64},{1,129},{65,193},{129,1},{193,65... | collective-permute-start | bytes 196616 | tf_op jit(solution)/shard_map/ppermute | solution.py:107
  8.6 11.6 %all-to-all-start = ((bf16[32,3,32,128]{3,2,1,0:T(8,128)(2,1)}), bf16[32,3,32,128]{3,2,1,0:T(8,128)(2,1)S(1)}, u32[]{:S(2)}, u32[]{:S(2)}) async-start(bf16[32,3,32,128]{3,2,1,0:T(8,128)(2,1)} %bitcast.44), calls=%async_computation | async-start | bytes 1572864 | tf_op jit(solution)/shard_map/all_to_all | solution.py:123
  27.6 15.2 %all-to-all-done = bf16[32,3,32,128]{3,2,1,0:T(8,128)(2,1)S(1)} async-done(((bf16[32,3,32,128]{3,2,1,0:T(8,128)(2,1)}), bf16[32,3,32,128]{3,2,1,0:T(8,128)(2,1)S(1)}, u32[]{:S(2)}, u32[]{:S(2)}) %all-to-all-start) | async-done | bytes 786464 | tf_op jit(solution)/shard_map/all_to_all | solution.py:123
  43.2 2.0 %collective-permute-start.11 = (bf16[96,4096]{1,0:T(8,128)(2,1)S(1)}, bf16[96,4096]{1,0:T(8,128)(2,1)S(1)}, u32[]{:S(2)}, u32[]{:S(2)}) collective-permute-start(bf16[96,4096]{1,0:T(8,128)(2,1)S(1)} %bitcast.46), channel_id=1, source_target_pairs={{0,64},{64,128},{128,192},{192,0},{1,65},{65,129},{129,193},{193,1... | collective-permute-start | bytes 2359304 | tf_op jit(solution)/shard_map/ppermute | solution.py:107
  45.2 1.9 %pad_maximum_fusion = bf16[4096,512]{1,0:T(8,128)(2,1)S(1)} fusion(bf16[4096,256]{1,0:T(8,128)(2,1)} %collective-permute-done.8, bf16[4096,256]{1,0:T(8,128)(2,1)S(1)} %bitcast.41), kind=kLoop, calls=%fused_computation.2 | loop fusion | flops 8388608 | bytes 8388608 | tf_op jit(solution)/shard_map/concatenate | solution.py:131
  47.2 1.9 %pad_maximum_fusion.1 = bf16[4096,512]{1,0:T(8,128)(2,1)S(1)} fusion(bf16[4096,256]{1,0:T(8,128)(2,1)} %collective-permute-done.9, bf16[4096,256]{1,0:T(8,128)(2,1)S(1)} %bitcast.43), kind=kLoop, calls=%fused_computation.3 | loop fusion | flops 8388608 | bytes 8388608 | tf_op jit(solution)/shard_map/concatenate | solution.py:131
  49.1 2.7 %pad_maximum_fusion.2 = bf16[512,4096]{1,0:T(8,128)(2,1)S(1)} fusion(bf16[256,4096]{1,0:T(8,128)(2,1)} %collective-permute-done.10, bf16[256,4096]{1,0:T(8,128)(2,1)} %bitcast.3), kind=kLoop, calls=%fused_computation.4 | loop fusion | flops 8388608 | bytes 8388608 | tf_op jit(solution)/shard_map/concatenate | solution.py:132
  51.8 10.4 %collective-permute-done.11 = bf16[96,4096]{1,0:T(8,128)(2,1)S(1)} collective-permute-done((bf16[96,4096]{1,0:T(8,128)(2,1)S(1)}, bf16[96,4096]{1,0:T(8,128)(2,1)S(1)}, u32[]{:S(2)}, u32[]{:S(2)}) %collective-permute-start.11) | collective-permute-done | bytes 786464 | tf_op jit(solution)/shard_map/ppermute | solution.py:107
  62.9 3.0 %collective-permute-start.14 = (bf16[48,4096]{1,0:T(8,128)(2,1)S(1)}, bf16[48,4096]{1,0:T(8,128)(2,1)S(1)}, u32[]{:S(2)}, u32[]{:S(2)}) collective-permute-start(bf16[48,4096]{1,0:T(8,128)(2,1)S(1)} %get-tuple-element.29), channel_id=1, source_target_pairs={{0,192},{64,0},{128,64},{192,128},{1,193},{65,1},{129,65},{193,129... | collective-permute-start | bytes 1179656 | tf_op jit(solution)/shard_map/ppermute | solution.py:107
  68.7 3.3 %collective-permute-done.13 = bf16[48,4096]{1,0:T(8,128)(2,1)S(1)} collective-permute-done((bf16[48,4096]{1,0:T(8,128)(2,1)S(1)}, bf16[48,4096]{1,0:T(8,128)(2,1)S(1)}, u32[]{:S(2)}, u32[]{:S(2)}) %collective-permute-start.13) | collective-permute-done | bytes 393248 | tf_op jit(solution)/shard_map/ppermute | solution.py:107
  74.7 1.8 %collective-permute-start.18 = (bf16[48,4096]{1,0:T(8,128)(2,1)S(1)}, bf16[48,4096]{1,0:T(8,128)(2,1)S(1)}, u32[]{:S(2)}, u32[]{:S(2)}) collective-permute-start(bf16[48,4096]{1,0:T(8,128)(2,1)S(1)} %get-tuple-element.24), channel_id=1, source_target_pairs={{0,64},{64,128},{128,192},{192,0},{1,65},{65,129},{129,193},{193,1... | collective-permute-start | bytes 1179656 | tf_op jit(solution)/shard_map/ppermute | solution.py:107
  77.2 1.6 %collective-permute-start.19 = (bf16[48,4096]{1,0:T(8,128)(2,1)S(1)}, bf16[48,4096]{1,0:T(8,128)(2,1)S(1)}, u32[]{:S(2)}, u32[]{:S(2)}) collective-permute-start(bf16[48,4096]{1,0:T(8,128)(2,1)S(1)} %get-tuple-element.25), channel_id=1, source_target_pairs={{0,192},{64,0},{128,64},{192,128},{1,193},{65,1},{129,65},{193,129... | collective-permute-start | bytes 1179656 | tf_op jit(solution)/shard_map/ppermute | solution.py:107
  78.9 8.7 %collective-permute-done.15 = bf16[48,4096]{1,0:T(8,128)(2,1)S(1)} collective-permute-done((bf16[48,4096]{1,0:T(8,128)(2,1)S(1)}, bf16[48,4096]{1,0:T(8,128)(2,1)S(1)}, u32[]{:S(2)}, u32[]{:S(2)}) %collective-permute-start.15) | collective-permute-done | bytes 393248 | tf_op jit(solution)/shard_map/ppermute | solution.py:107
  93.2 1.7 %collective-permute-done.18 = bf16[48,4096]{1,0:T(8,128)(2,1)S(1)} collective-permute-done((bf16[48,4096]{1,0:T(8,128)(2,1)S(1)}, bf16[48,4096]{1,0:T(8,128)(2,1)S(1)}, u32[]{:S(2)}, u32[]{:S(2)}) %collective-permute-start.18) | collective-permute-done | bytes 393248 | tf_op jit(solution)/shard_map/ppermute | solution.py:107
  94.9 3.8 %collective-permute-done.20 = bf16[48,4096]{1,0:T(8,128)(2,1)S(1)} collective-permute-done((bf16[48,4096]{1,0:T(8,128)(2,1)S(1)}, bf16[48,4096]{1,0:T(8,128)(2,1)S(1)}, u32[]{:S(2)}, u32[]{:S(2)}) %collective-permute-start.20) | collective-permute-done | bytes 393248 | tf_op jit(solution)/shard_map/ppermute | solution.py:107
  98.7 4.1 %collective-permute-done.17 = bf16[48,4096]{1,0:T(8,128)(2,1)S(1)} collective-permute-done((bf16[48,4096]{1,0:T(8,128)(2,1)S(1)}, bf16[48,4096]{1,0:T(8,128)(2,1)S(1)}, u32[]{:S(2)}, u32[]{:S(2)}) %collective-permute-start.17) | collective-permute-done | bytes 393248 | tf_op jit(solution)/shard_map/ppermute | solution.py:107
  104.9 7.8 %all-to-all-start.1 = ((bf16[32,3,32,128]{3,2,1,0:T(8,128)(2,1)}), bf16[32,3,32,128]{3,2,1,0:T(8,128)(2,1)S(1)}, u32[]{:S(2)}, u32[]{:S(2)}) async-start(bf16[32,3,32,128]{3,2,1,0:T(8,128)(2,1)} %bitcast.10), calls=%async_computation.1 | async-start | bytes 1572864 | tf_op jit(solution)/shard_map/all_to_all | solution.py:123
  112.7 1.8 %collective-permute-start.7 = (bf16[8,4096]{1,0:T(8,128)(2,1)S(1)}, bf16[8,4096]{1,0:T(8,128)(2,1)S(1)}, u32[]{:S(2)}, u32[]{:S(2)}) collective-permute-start(bf16[8,4096]{1,0:T(8,128)(2,1)S(1)} %get-tuple-element.32), channel_id=1, source_target_pairs={{0,64},{64,128},{128,192},{192,0},{1,65},{65,129},{129,193},{193,1... | collective-permute-start | bytes 196616 | tf_op jit(solution)/shard_map/ppermute | solution.py:107
  114.6 2.5 %collective-permute-start.6 = (bf16[8,4096]{1,0:T(8,128)(2,1)S(1)}, bf16[8,4096]{1,0:T(8,128)(2,1)S(1)}, u32[]{:S(2)}, u32[]{:S(2)}) collective-permute-start(bf16[8,4096]{1,0:T(8,128)(2,1)S(1)} %get-tuple-element.33), channel_id=1, source_target_pairs={{0,128},{64,192},{128,0},{192,64},{1,129},{65,193},{129,1},{193,65... | collective-permute-start | bytes 196616 | tf_op jit(solution)/shard_map/ppermute | solution.py:107
  118.3 2.0 %collective-permute-done.6 = bf16[8,4096]{1,0:T(8,128)(2,1)S(1)} collective-permute-done((bf16[8,4096]{1,0:T(8,128)(2,1)S(1)}, bf16[8,4096]{1,0:T(8,128)(2,1)S(1)}, u32[]{:S(2)}, u32[]{:S(2)}) %collective-permute-start.6) | collective-permute-done | bytes 65568 | tf_op jit(solution)/shard_map/ppermute | solution.py:107
  121.4 9.0 %all-to-all-done.1 = bf16[32,3,32,128]{3,2,1,0:T(8,128)(2,1)S(1)} async-done(((bf16[32,3,32,128]{3,2,1,0:T(8,128)(2,1)}), bf16[32,3,32,128]{3,2,1,0:T(8,128)(2,1)S(1)}, u32[]{:S(2)}, u32[]{:S(2)}) %all-to-all-start.1) | async-done | bytes 786464 | tf_op jit(solution)/shard_map/all_to_all | solution.py:123
  130.4 1.5 %combine_rows.1 = bf16[8,4096]{1,0:T(8,128)(2,1)} custom-call(s32[8,8]{1,0:T(8,128)S(1)} %copy-done.1, f32[8,8]{1,0:T(8,128)S(1)} %copy-done, f32[8,4096]{1,0:T(8,128)S(1)} %fusion.8.shared_ref, bf16[96,32,128]{2,1,0:T(8,128)(2,1)S(1)} %bitcast.36), custom_call_target="tpu_custom_call" | custom-call | tf_op jit(solution)/shard_map/combine_rows/pallas_call | solution.py:84
  (78 shorter events, 26.5 us)
Async XLA Ops:
  2.1 19.0 %collective-permute-start = (bf16[8,4096]{1,0:T(8,128)(2,1)}, bf16[8,4096]{1,0:T(8,128)(2,1)S(1)}, u32[]{:S(2)}, u32[]{:S(2)}) collective-permute-start(bf16[8,4096]{1,0:T(8,128)(2,1)} %rows_hbm.1), channel_id=1, source_target_pairs={{0,64},{64,128},{128,192},{192,0},{1,65},{65,129},{129,193},{193,1... | collective-permute-start | bytes 196616 | tf_op jit(solution)/shard_map/ppermute | solution.py:107
  3.8 17.4 %collective-permute-start.1 = (bf16[8,4096]{1,0:T(8,128)(2,1)}, bf16[8,4096]{1,0:T(8,128)(2,1)S(1)}, u32[]{:S(2)}, u32[]{:S(2)}) collective-permute-start(bf16[8,4096]{1,0:T(8,128)(2,1)} %rows_hbm.1), channel_id=1, source_target_pairs={{0,128},{64,192},{128,0},{192,64},{1,129},{65,193},{129,1},{193,65... | collective-permute-start | bytes 196616 | tf_op jit(solution)/shard_map/ppermute | solution.py:107
  6.7 14.5 %collective-permute-start.2 = (bf16[8,4096]{1,0:T(8,128)(2,1)}, bf16[8,4096]{1,0:T(8,128)(2,1)}, u32[]{:S(2)}, u32[]{:S(2)}) collective-permute-start(bf16[8,4096]{1,0:T(8,128)(2,1)} %rows_hbm.1), channel_id=1, source_target_pairs={{0,192},{64,0},{128,64},{192,128},{1,193},{65,1},{129,65},{193,129... | collective-permute-start | bytes 196616 | tf_op jit(solution)/shard_map/ppermute | solution.py:107
  8.0 37.2 %collective-permute-start.8 = (bf16[4096,256]{1,0:T(8,128)(2,1)}, bf16[4096,256]{1,0:T(8,128)(2,1)}, u32[]{:S(2)}, u32[]{:S(2)}) collective-permute-start(bf16[4096,256]{1,0:T(8,128)(2,1)} %bitcast.40), channel_id=1, source_target_pairs={{0,32},{32,0},{1,33},{33,1},{2,34},{34,2},{3,35},{35,3},{4,36},{36... | collective-permute-start | bytes 6291464 | tf_op jit(solution)/shard_map/ppermute | solution.py:107
  8.1 39.1 %collective-permute-start.9 = (bf16[4096,256]{1,0:T(8,128)(2,1)}, bf16[4096,256]{1,0:T(8,128)(2,1)}, u32[]{:S(2)}, u32[]{:S(2)}) collective-permute-start(bf16[4096,256]{1,0:T(8,128)(2,1)} %bitcast.42), channel_id=1, source_target_pairs={{0,32},{32,0},{1,33},{33,1},{2,34},{34,2},{3,35},{35,3},{4,36},{36... | collective-permute-start | bytes 6291464 | tf_op jit(solution)/shard_map/ppermute | solution.py:107
  8.6 34.2 %all-to-all-start = ((bf16[32,3,32,128]{3,2,1,0:T(8,128)(2,1)}), bf16[32,3,32,128]{3,2,1,0:T(8,128)(2,1)S(1)}, u32[]{:S(2)}, u32[]{:S(2)}) async-start(bf16[32,3,32,128]{3,2,1,0:T(8,128)(2,1)} %bitcast.44), calls=%async_computation | async-start | bytes 1572864 | tf_op jit(solution)/shard_map/all_to_all | solution.py:123
  22.1 1.6 %collective-permute-start.3 = (bf16[32,4096]{1,0:T(8,128)(2,1)S(1)}, bf16[32,4096]{1,0:T(8,128)(2,1)S(1)}, u32[]{:S(2)}, u32[]{:S(2)}) collective-permute-start(bf16[32,4096]{1,0:T(8,128)(2,1)S(1)} %pad_maximum_fusion.8), channel_id=1, source_target_pairs={{0,32},{32,0},{1,33},{33,1},{2,34},{34,2},{3,35},{35,3},{4,36},{36... | collective-permute-start | bytes 786440 | tf_op jit(solution)/shard_map/ppermute | solution.py:107
  25.3 1.6 %collective-permute-start.4 = (bf16[32,4096]{1,0:T(8,128)(2,1)S(1)}, bf16[32,4096]{1,0:T(8,128)(2,1)S(1)}, u32[]{:S(2)}, u32[]{:S(2)}) collective-permute-start(bf16[32,4096]{1,0:T(8,128)(2,1)S(1)} %slice.117), channel_id=1, source_target_pairs={{0,32},{32,0},{1,33},{33,1},{2,34},{34,2},{3,35},{35,3},{4,36},{36... | collective-permute-start | bytes 786440 | tf_op jit(solution)/shard_map/ppermute | solution.py:107
  25.5 23.6 %collective-permute-start.10 = (bf16[256,4096]{1,0:T(8,128)(2,1)}, bf16[256,4096]{1,0:T(8,128)(2,1)}, u32[]{:S(2)}, u32[]{:S(2)}) collective-permute-start(bf16[256,4096]{1,0:T(8,128)(2,1)} %bitcast.3), channel_id=1, source_target_pairs={{0,32},{32,0},{1,33},{33,1},{2,34},{34,2},{3,35},{35,3},{4,36},{36... | collective-permute-start | bytes 6291464 | tf_op jit(solution)/shard_map/ppermute | solution.py:107
  43.1 19.7 %collective-permute-start.12 = (bf16[96,4096]{1,0:T(8,128)(2,1)S(1)}, bf16[96,4096]{1,0:T(8,128)(2,1)S(1)}, u32[]{:S(2)}, u32[]{:S(2)}) collective-permute-start(bf16[96,4096]{1,0:T(8,128)(2,1)S(1)} %bitcast.45), channel_id=1, source_target_pairs={{0,192},{64,0},{128,64},{192,128},{1,193},{65,1},{129,65},{193,129... | collective-permute-start | bytes 2359304 | tf_op jit(solution)/shard_map/ppermute | solution.py:107
  43.2 19.0 %collective-permute-start.11 = (bf16[96,4096]{1,0:T(8,128)(2,1)S(1)}, bf16[96,4096]{1,0:T(8,128)(2,1)S(1)}, u32[]{:S(2)}, u32[]{:S(2)}) collective-permute-start(bf16[96,4096]{1,0:T(8,128)(2,1)S(1)} %bitcast.46), channel_id=1, source_target_pairs={{0,64},{64,128},{128,192},{192,0},{1,65},{65,129},{129,193},{193,1... | collective-permute-start | bytes 2359304 | tf_op jit(solution)/shard_map/ppermute | solution.py:107
  62.2 9.7 %collective-permute-start.13 = (bf16[48,4096]{1,0:T(8,128)(2,1)S(1)}, bf16[48,4096]{1,0:T(8,128)(2,1)S(1)}, u32[]{:S(2)}, u32[]{:S(2)}) collective-permute-start(bf16[48,4096]{1,0:T(8,128)(2,1)S(1)} %get-tuple-element.27), channel_id=1, source_target_pairs={{0,64},{64,128},{128,192},{192,0},{1,65},{65,129},{129,193},{193,1... | collective-permute-start | bytes 1179656 | tf_op jit(solution)/shard_map/ppermute | solution.py:107
  62.9 9.1 %collective-permute-start.14 = (bf16[48,4096]{1,0:T(8,128)(2,1)S(1)}, bf16[48,4096]{1,0:T(8,128)(2,1)S(1)}, u32[]{:S(2)}, u32[]{:S(2)}) collective-permute-start(bf16[48,4096]{1,0:T(8,128)(2,1)S(1)} %get-tuple-element.29), channel_id=1, source_target_pairs={{0,192},{64,0},{128,64},{192,128},{1,193},{65,1},{129,65},{193,129... | collective-permute-start | bytes 1179656 | tf_op jit(solution)/shard_map/ppermute | solution.py:107
  74.5 13.0 %collective-permute-start.15 = (bf16[48,4096]{1,0:T(8,128)(2,1)S(1)}, bf16[48,4096]{1,0:T(8,128)(2,1)S(1)}, u32[]{:S(2)}, u32[]{:S(2)}) collective-permute-start(bf16[48,4096]{1,0:T(8,128)(2,1)S(1)} %get-tuple-element.26), channel_id=1, source_target_pairs={{0,64},{64,128},{128,192},{192,0},{1,65},{65,129},{129,193},{193,1... | collective-permute-start | bytes 1179656 | tf_op jit(solution)/shard_map/ppermute | solution.py:107
  74.7 20.2 %collective-permute-start.18 = (bf16[48,4096]{1,0:T(8,128)(2,1)S(1)}, bf16[48,4096]{1,0:T(8,128)(2,1)S(1)}, u32[]{:S(2)}, u32[]{:S(2)}) collective-permute-start(bf16[48,4096]{1,0:T(8,128)(2,1)S(1)} %get-tuple-element.24), channel_id=1, source_target_pairs={{0,64},{64,128},{128,192},{192,0},{1,65},{65,129},{129,193},{193,1... | collective-permute-start | bytes 1179656 | tf_op jit(solution)/shard_map/ppermute | solution.py:107
  77.2 10.9 %collective-permute-start.19 = (bf16[48,4096]{1,0:T(8,128)(2,1)S(1)}, bf16[48,4096]{1,0:T(8,128)(2,1)S(1)}, u32[]{:S(2)}, u32[]{:S(2)}) collective-permute-start(bf16[48,4096]{1,0:T(8,128)(2,1)S(1)} %get-tuple-element.25), channel_id=1, source_target_pairs={{0,192},{64,0},{128,64},{192,128},{1,193},{65,1},{129,65},{193,129... | collective-permute-start | bytes 1179656 | tf_op jit(solution)/shard_map/ppermute | solution.py:107
  88.2 10.4 %collective-permute-start.20 = (bf16[48,4096]{1,0:T(8,128)(2,1)S(1)}, bf16[48,4096]{1,0:T(8,128)(2,1)S(1)}, u32[]{:S(2)}, u32[]{:S(2)}) collective-permute-start(bf16[48,4096]{1,0:T(8,128)(2,1)S(1)} %fusion.3), channel_id=1, source_target_pairs={{0,192},{64,0},{128,64},{192,128},{1,193},{65,1},{129,65},{193,129... | collective-permute-start | bytes 1179656 | tf_op jit(solution)/shard_map/ppermute | solution.py:107
  91.1 11.8 %collective-permute-start.17 = (bf16[48,4096]{1,0:T(8,128)(2,1)S(1)}, bf16[48,4096]{1,0:T(8,128)(2,1)S(1)}, u32[]{:S(2)}, u32[]{:S(2)}) collective-permute-start(bf16[48,4096]{1,0:T(8,128)(2,1)S(1)} %get-tuple-element.23), channel_id=1, source_target_pairs={{0,192},{64,0},{128,64},{192,128},{1,193},{65,1},{129,65},{193,129... | collective-permute-start | bytes 1179656 | tf_op jit(solution)/shard_map/ppermute | solution.py:107
  92.4 10.4 %collective-permute-start.16 = (bf16[48,4096]{1,0:T(8,128)(2,1)S(1)}, bf16[48,4096]{1,0:T(8,128)(2,1)S(1)}, u32[]{:S(2)}, u32[]{:S(2)}) collective-permute-start(bf16[48,4096]{1,0:T(8,128)(2,1)S(1)} %fusion.4), channel_id=1, source_target_pairs={{0,64},{64,128},{128,192},{192,0},{1,65},{65,129},{129,193},{193,1... | collective-permute-start | bytes 1179656 | tf_op jit(solution)/shard_map/ppermute | solution.py:107
  103.8 26.6 %copy-start = (f32[8,8]{1,0:T(8,128)S(1)}, f32[8,8]{1,0:T(8,128)}, u32[]{:S(2)}) copy-start(f32[8,8]{1,0:T(8,128)} %gates_ref.1) | copy-start | bytes 772
  104.9 25.5 %all-to-all-start.1 = ((bf16[32,3,32,128]{3,2,1,0:T(8,128)(2,1)}), bf16[32,3,32,128]{3,2,1,0:T(8,128)(2,1)S(1)}, u32[]{:S(2)}, u32[]{:S(2)}) async-start(bf16[32,3,32,128]{3,2,1,0:T(8,128)(2,1)} %bitcast.10), calls=%async_computation.1 | async-start | bytes 1572864 | tf_op jit(solution)/shard_map/all_to_all | solution.py:123
  112.7 5.6 %collective-permute-start.7 = (bf16[8,4096]{1,0:T(8,128)(2,1)S(1)}, bf16[8,4096]{1,0:T(8,128)(2,1)S(1)}, u32[]{:S(2)}, u32[]{:S(2)}) collective-permute-start(bf16[8,4096]{1,0:T(8,128)(2,1)S(1)} %get-tuple-element.32), channel_id=1, source_target_pairs={{0,64},{64,128},{128,192},{192,0},{1,65},{65,129},{129,193},{193,1... | collective-permute-start | bytes 196616 | tf_op jit(solution)/shard_map/ppermute | solution.py:107
  114.6 5.8 %collective-permute-start.6 = (bf16[8,4096]{1,0:T(8,128)(2,1)S(1)}, bf16[8,4096]{1,0:T(8,128)(2,1)S(1)}, u32[]{:S(2)}, u32[]{:S(2)}) collective-permute-start(bf16[8,4096]{1,0:T(8,128)(2,1)S(1)} %get-tuple-element.33), channel_id=1, source_target_pairs={{0,128},{64,192},{128,0},{192,64},{1,129},{65,193},{129,1},{193,65... | collective-permute-start | bytes 196616 | tf_op jit(solution)/shard_map/ppermute | solution.py:107
  117.1 4.3 %collective-permute-start.5 = (bf16[8,4096]{1,0:T(8,128)(2,1)S(1)}, bf16[8,4096]{1,0:T(8,128)(2,1)S(1)}, u32[]{:S(2)}, u32[]{:S(2)}) collective-permute-start(bf16[8,4096]{1,0:T(8,128)(2,1)S(1)} %get-tuple-element.31), channel_id=1, source_target_pairs={{0,192},{64,0},{128,64},{192,128},{1,193},{65,1},{129,65},{193,129... | collective-permute-start | bytes 196616 | tf_op jit(solution)/shard_map/ppermute | solution.py:107
  (7 other events, 88.3 us)
